TPU v7x, 32 devices: a whole 2x2x4 slice. The times are simulated.
32 devices in a mesh: rep: 16 (over z, y, core), fsdp: 2 (over x).
Axes of the slice: x: 2, y: 2, z: 4, core: 2. Of those that a mesh axis runs over, the one named last changes fastest.
Arguments:
- tokens: bfloat16 [2, 16, 1024, 768], P(None, 'rep', 'fsdp'), may hold values from -6 to 6
- cotangent: bfloat16 [2, 16, 1024, 768], P(None, 'rep', 'fsdp'), may hold values from -6 to 6
- doc_ids: int32 [2, 16, 1024], P(None, 'rep'), may hold values from 0 to 3, never falling along the last dimension, each value on 1 to 512 neighbouring positions
- positions: int32 [2, 16, 128], P(None, 'rep'), may hold values from 0 to 1023, as said below
- w_qkv: bfloat16 [768, 2304], P('fsdp'), may hold values from -0.21875 to 0.21875
- w_out: bfloat16 [768, 768], P('fsdp'), may hold values from -0.625 to 0.625
- w_fc: bfloat16 [768, 3072], P('fsdp'), may hold values from -0.21875 to 0.21875
- w_proj: bfloat16 [3072, 768], P('fsdp'), may hold values from -0.109375 to 0.109375
- ln1_gain: bfloat16 [768], P('fsdp'), may hold values from 0.5 to 1.5
- ln1_bias: bfloat16 [768], P('fsdp'), may hold values from -0.796875 to 0.796875
- ln2_gain: bfloat16 [768], P('fsdp'), may hold values from 0.5 to 1.5
- ln2_bias: bfloat16 [768], P('fsdp'), may hold values from -0.796875 to 0.796875
- fc_bias: bfloat16 [3072], P('fsdp'), may hold values from -0.796875 to 0.796875
- proj_bias: bfloat16 [768], P('fsdp'), may hold values from -0.796875 to 0.796875
- mean_weight: bfloat16 [256, 12], P('fsdp'), may hold values from -0.375 to 0.375
- spread_weight: bfloat16 [256, 12], P('fsdp'), may hold values from -0.375 to 0.375
Outputs:
- output: bfloat16 [2, 16, 1024, 768], P(None, 'rep', 'fsdp')
- grad_tokens: float32 [2, 16, 1024, 768], P(None, 'rep', 'fsdp')
- grad_w_qkv: float32 [768, 2304], P('fsdp')
- grad_w_out: float32 [768, 768], P('fsdp')
- grad_w_fc: float32 [768, 3072], P('fsdp')
- grad_w_proj: float32 [3072, 768], P('fsdp')
- grad_ln1_gain: float32 [768], P('fsdp')
- grad_ln1_bias: float32 [768], P('fsdp')
- grad_ln2_gain: float32 [768], P('fsdp')
- grad_ln2_bias: float32 [768], P('fsdp')
- grad_fc_bias: float32 [3072], P('fsdp')
- grad_proj_bias: float32 [768], P('fsdp')
- grad_mean_weight: float32 [256, 12], P('fsdp')
- grad_spread_weight: float32 [256, 12], P('fsdp')
Inputs may be any that keep to these rules, and one draw needn't show every extreme that they name: `positions`: samples 64 * j to 64 * (j + 1) - 1 of a sequence are distinct tokens of its j-th run of 512 tokens, among them the run's first and last token. `doc_ids`: A sequence's document numbers never fall along it; a document has at most 512 tokens.
All inputs are finite; a program needn't handle non-finite values.
Results may differ from a plain program's by a relative error of at most 0.019.
Values may be sent and summed in bfloat16 or wider, within the bound.
No kernel may reach another device: no remote copies, remote signals or barrier semaphores. Data moves between devices by JAX's collectives and lax.ppermute only.
A program may use at most 320 MiB of HBM per device.

v0:
```python
from functools import partial

import jax
import jax.numpy as jnp
from jax import lax
from jax.sharding import PartitionSpec as P

BLK = 256


HIGHEST = lax.Precision.HIGHEST
EPSILON = 1e-05
RIDGE_TERM = 0.5
SIGMA_SCALE = 0.01
MASKED = -1e30


def shifted(value, axis, by):
    peers = lax.axis_size(axis)
    pairs = [(i, i + by) for i in range(peers) if 0 <= i + by < peers]
    return lax.ppermute(value, axis, pairs)


def layer_norm(inputs, gains, offsets):
    centred = inputs - jnp.mean(inputs, axis=-1, keepdims=True)
    inv_std = lax.rsqrt(jnp.mean(centred * centred, axis=-1, keepdims=True) + EPSILON)
    normed = centred * inv_std
    return (normed * gains + offsets, normed, inv_std)


def norm_back(grad_out, normed, inv_std, gains):
    grad_norm = grad_out * gains
    centred_grad = (
        grad_norm
        - jnp.mean(grad_norm, axis=-1, keepdims=True)
        - normed * jnp.mean(grad_norm * normed, axis=-1, keepdims=True)
    )
    return (inv_std * centred_grad, jnp.sum(grad_out * normed, axis=0), jnp.sum(grad_out, axis=0))


def contract_rows(first_op, second_op):
    return lax.dot_general(
        first_op, second_op, (((0,), (0,)), ((), ())), preferred_element_type=jnp.float32
    )


def contract_cols(first_op, second_op):
    return lax.dot_general(
        first_op, second_op, (((1,), (1,)), ((), ())), preferred_element_type=jnp.float32
    )


def basis_rows(sample_pos, length, basis_count):
    times = (sample_pos.astype(jnp.float32) + 0.5) / length
    centres = (jnp.arange(basis_count, dtype=jnp.float32) + 0.5) / basis_count
    basis_width = 1.25 / basis_count
    return jnp.exp(-((times[:, None] - centres[None, :]) ** 2) / (2.0 * basis_width * basis_width))


def density_weights(scaled, mean_proj, spread_proj, basis_count):
    centres = (jnp.arange(basis_count, dtype=jnp.float32) + 0.5) / basis_count
    basis_var = (1.25 / basis_count) ** 2
    mean_logit = jnp.einsum("thn,nh->th", scaled, mean_proj, precision=HIGHEST)
    spread_logit = jnp.einsum("thn,nh->th", scaled, spread_proj, precision=HIGHEST)
    middle = jax.nn.sigmoid(mean_logit)
    spread_sq = basis_var + SIGMA_SCALE * jax.nn.softplus(spread_logit)
    amplitude = jnp.sqrt(basis_var / spread_sq)
    offset_sq = (middle[..., None] - centres) ** 2
    return amplitude[..., None] * jnp.exp(-offset_sq / (2.0 * spread_sq[..., None]))


def block_pattern(block):
    query_blk = jnp.arange(2 * block) // block + 1
    key_blk = jnp.arange(3 * block) // block
    return (key_blk[None, :] == query_blk[:, None]) | (key_blk[None, :] == query_blk[:, None] - 1)


def block_probs(q_part, key_part, allowed, score_scale):
    raw_scores = (
        jnp.einsum("qhd,khd->hqk", q_part, key_part, preferred_element_type=jnp.float32)
        * score_scale
    )
    return jnp.where(allowed[None], raw_scores, MASKED)


def on_device(
    tokens,
    cotangent,
    doc_ids,
    positions,
    w_qkv,
    w_out,
    w_fc,
    w_proj,
    ln1_gain,
    ln1_bias,
    ln2_gain,
    ln2_bias,
    fc_bias,
    proj_bias,
    mean_weight,
    spread_weight,
):
    group_size = lax.axis_size("fsdp")
    member = lax.axis_index("fsdp")
    micro_count = tokens.shape[0]
    tok_rows = tokens.shape[2]
    model_dim = tokens.shape[3]
    hidden_dim = w_fc.shape[1]
    head_count = mean_weight.shape[1]
    basis_count = mean_weight.shape[0] * group_size
    head_dim = model_dim // head_count
    score_scale = head_dim ** (-0.5)
    block = BLK
    rows_group = 2 * block
    seq_len = tok_rows * group_size
    sample_dev = positions.shape[2] // group_size
    first_row = member * tok_rows
    pattern = block_pattern(block)
    gathered = (
        lax.all_gather(w_qkv, "fsdp", axis=0, tiled=True),
        lax.all_gather(w_out, "fsdp", axis=0, tiled=True),
        lax.all_gather(w_fc, "fsdp", axis=0, tiled=True),
        lax.all_gather(w_proj, "fsdp", axis=0, tiled=True),
        lax.all_gather(ln1_gain, "fsdp", axis=0, tiled=True),
        lax.all_gather(ln1_bias, "fsdp", axis=0, tiled=True),
        lax.all_gather(ln2_gain, "fsdp", axis=0, tiled=True),
        lax.all_gather(ln2_bias, "fsdp", axis=0, tiled=True),
        lax.all_gather(fc_bias, "fsdp", axis=0, tiled=True),
        lax.all_gather(proj_bias, "fsdp", axis=0, tiled=True),
        lax.all_gather(mean_weight, "fsdp", axis=0, tiled=True),
        lax.all_gather(spread_weight, "fsdp", axis=0, tiled=True),
    )
    acc_qkv = jnp.zeros((model_dim, 3 * model_dim), jnp.float32)
    acc_out = jnp.zeros((model_dim, model_dim), jnp.float32)
    acc_fc = jnp.zeros((model_dim, hidden_dim), jnp.float32)
    acc_proj = jnp.zeros((hidden_dim, model_dim), jnp.float32)
    acc_gain_one = jnp.zeros((model_dim,), jnp.float32)
    acc_bias_one = jnp.zeros((model_dim,), jnp.float32)
    acc_gain_two = jnp.zeros((model_dim,), jnp.float32)
    acc_bias_two = jnp.zeros((model_dim,), jnp.float32)
    acc_hidden = jnp.zeros((hidden_dim,), jnp.float32)
    acc_output = jnp.zeros((model_dim,), jnp.float32)
    acc_mean = jnp.zeros((basis_count, head_count), jnp.float32)
    acc_spread = jnp.zeros((basis_count, head_count), jnp.float32)
    outputs_list = []
    grads_list = []
    for micro_idx in range(micro_count):
        (
            full_qkv,
            full_out,
            full_fc,
            full_proj,
            gain_first,
            bias_first,
            gain_second,
            bias_second,
            hidden_bias,
            output_bias,
            mean_proj,
            spread_proj,
        ) = gathered
        gain_first = gain_first.astype(jnp.float32)
        bias_first = bias_first.astype(jnp.float32)
        gain_second = gain_second.astype(jnp.float32)
        bias_second = bias_second.astype(jnp.float32)
        hidden_bias = hidden_bias.astype(jnp.float32)
        output_bias = output_bias.astype(jnp.float32)
        mean_f32 = mean_proj.astype(jnp.float32)
        spread_f32 = spread_proj.astype(jnp.float32)
        inputs = tokens[micro_idx, 0].astype(jnp.float32)
        seq_docs = doc_ids[micro_idx, 0]
        sample_pos = positions[micro_idx, 0]
        first_norm, normed_one, inv_one = layer_norm(inputs, gain_first, bias_first)
        first_low = first_norm.astype(jnp.bfloat16)
        qkv_low = jnp.dot(first_low, full_qkv, preferred_element_type=jnp.float32).astype(
            jnp.bfloat16
        )
        queries = qkv_low[:, :model_dim].reshape(tok_rows, head_count, head_dim)
        keyval = qkv_low[:, model_dim:]
        earlier = shifted(keyval[tok_rows - block :], "fsdp", 1)
        extended = jnp.concatenate([earlier, keyval], axis=0)
        padded_docs = jnp.concatenate([jnp.full((block,), -1, jnp.int32), seq_docs])
        ext_docs = lax.dynamic_slice_in_dim(padded_docs, first_row, tok_rows + block)
        own_docs = lax.dynamic_slice_in_dim(seq_docs, first_row, tok_rows)
        basis_tab = basis_rows(sample_pos, seq_len, basis_count)
        system = jnp.dot(
            basis_tab.T, basis_tab, precision=HIGHEST, preferred_element_type=jnp.float32
        )
        system = system + RIDGE_TERM * jnp.eye(basis_count, dtype=jnp.float32)
        factor = jnp.linalg.cholesky(system)
        own_basis = lax.dynamic_slice_in_dim(basis_tab, member * sample_dev, sample_dev)
        own_rows = lax.dynamic_slice_in_dim(sample_pos, member * sample_dev, sample_dev) - first_row
        picked = jnp.take(first_low, own_rows, axis=0).astype(jnp.float32)
        partial_fit = jnp.dot(
            own_basis.T, picked, precision=HIGHEST, preferred_element_type=jnp.float32
        )
        fitted = lax.psum(partial_fit, "fsdp")
        coeffs = jax.scipy.linalg.cho_solve((factor, True), fitted)
        coeff_low = coeffs.astype(jnp.bfloat16)
        memory_kv = jnp.dot(
            coeff_low, full_qkv[:, model_dim:], preferred_element_type=jnp.float32
        ).astype(jnp.bfloat16)
        mem_keys = memory_kv[:, :model_dim].reshape(basis_count, head_count, head_dim)
        mem_vals = memory_kv[:, model_dim:].reshape(basis_count, head_count, head_dim)
        scaled = (
            jnp.einsum("thd,nhd->thn", queries, mem_keys, preferred_element_type=jnp.float32)
            * score_scale
        )
        density, density_back = jax.vjp(
            partial(density_weights, basis_count=basis_count), scaled, mean_f32, spread_f32
        )
        density_low = density.astype(jnp.bfloat16)
        mem_out = jnp.einsum(
            "thn,nhd->thd", density_low, mem_vals, preferred_element_type=jnp.float32
        )
        group_idx = 0
        row_lo = group_idx * rows_group
        q_part = queries
        kv_part = extended
        key_part = kv_part[:, :model_dim].reshape(-1, head_count, head_dim)
        val_part = kv_part[:, model_dim:].reshape(-1, head_count, head_dim)
        allowed = pattern & (
            own_docs[row_lo : row_lo + rows_group, None]
            == ext_docs[None, row_lo : row_lo + rows_group + block]
        )
        masked = block_probs(q_part, key_part, allowed, score_scale)
        log_total = jax.nn.logsumexp(masked, axis=-1, keepdims=True)
        attn_prob = jnp.exp(masked - log_total).astype(jnp.bfloat16)
        attn_parts = jnp.einsum(
            "hqk,khd->qhd", attn_prob, val_part, preferred_element_type=jnp.float32
        )
        log_totals = [log_total]
        context_low = (attn_parts + mem_out).reshape(tok_rows, model_dim).astype(jnp.bfloat16)
        branch_out = jnp.dot(context_low, full_out, preferred_element_type=jnp.float32)
        residual = inputs + branch_out
        second_norm, normed_two, inv_two = layer_norm(residual, gain_second, bias_second)
        second_low = second_norm.astype(jnp.bfloat16)
        pre_act = jnp.dot(second_low, full_fc, preferred_element_type=jnp.float32) + hidden_bias
        activated, gelu_back = jax.vjp(partial(jax.nn.gelu, approximate=True), pre_act)
        act_low = activated.astype(jnp.bfloat16)
        mlp_out = jnp.dot(act_low, full_proj, preferred_element_type=jnp.float32) + output_bias
        outputs_list.append((residual + mlp_out).astype(jnp.bfloat16))
        grad_out = cotangent[micro_idx, 0].astype(jnp.float32)
        grad_mlp = grad_out.astype(jnp.bfloat16)
        acc_proj = acc_proj + contract_rows(act_low, grad_mlp)
        acc_output = acc_output + jnp.sum(grad_mlp.astype(jnp.float32), axis=0)
        grad_act = contract_cols(grad_mlp, full_proj)
        grad_pre = gelu_back(grad_act)[0].astype(jnp.bfloat16)
        acc_hidden = acc_hidden + jnp.sum(grad_pre.astype(jnp.float32), axis=0)
        acc_fc = acc_fc + contract_rows(second_low, grad_pre)
        grad_second = contract_cols(grad_pre, full_fc)
        grad_resid_ln, gain_two_term, bias_two_term = norm_back(
            grad_second, normed_two, inv_two, gain_second
        )
        acc_gain_two = acc_gain_two + gain_two_term
        acc_bias_two = acc_bias_two + bias_two_term
        grad_resid = grad_out + grad_resid_ln
        grad_branch = grad_resid.astype(jnp.bfloat16)
        acc_out = acc_out + contract_rows(context_low, grad_branch)
        grad_context = contract_cols(grad_branch, full_out).astype(jnp.bfloat16)
        grad_ctx3 = grad_context.reshape(tok_rows, head_count, head_dim)
        grad_density = jnp.einsum(
            "thd,nhd->thn", grad_ctx3, mem_vals, preferred_element_type=jnp.float32
        )
        grad_memvals = jnp.einsum(
            "thn,thd->nhd", density_low, grad_ctx3, preferred_element_type=jnp.float32
        )
        grad_scaled, grad_meanw, grad_spreadw = density_back(grad_density)
        acc_mean = acc_mean + grad_meanw
        acc_spread = acc_spread + grad_spreadw
        scaled_grad_low = grad_scaled.astype(jnp.bfloat16)
        grad_query_mem = (
            jnp.einsum(
                "thn,nhd->thd", scaled_grad_low, mem_keys, preferred_element_type=jnp.float32
            )
            * score_scale
        )
        grad_memkeys = (
            jnp.einsum("thn,thd->nhd", scaled_grad_low, queries, preferred_element_type=jnp.float32)
            * score_scale
        )
        grad_ext = jnp.zeros((tok_rows + block, 2 * model_dim), jnp.float32)
        group_idx = 0
        row_lo = group_idx * rows_group
        q_part = queries
        kv_part = extended
        key_part = kv_part[:, :model_dim].reshape(-1, head_count, head_dim)
        val_part = kv_part[:, model_dim:].reshape(-1, head_count, head_dim)
        allowed = pattern & (
            own_docs[row_lo : row_lo + rows_group, None]
            == ext_docs[None, row_lo : row_lo + rows_group + block]
        )
        masked = block_probs(q_part, key_part, allowed, score_scale)
        attn_prob = jnp.exp(masked - log_totals[group_idx])
        grad_prob = jnp.einsum(
            "qhd,khd->hqk", grad_ctx3, val_part, preferred_element_type=jnp.float32
        )
        row_dot = jnp.sum(grad_prob * attn_prob, axis=-1, keepdims=True)
        grad_scores = (attn_prob * (grad_prob - row_dot)).astype(jnp.bfloat16)
        query_parts = (
            jnp.einsum("hqk,khd->qhd", grad_scores, key_part, preferred_element_type=jnp.float32)
            * score_scale
        )
        grad_keys = (
            jnp.einsum("hqk,qhd->khd", grad_scores, q_part, preferred_element_type=jnp.float32)
            * score_scale
        )
        grad_vals = jnp.einsum(
            "hqk,qhd->khd",
            attn_prob.astype(jnp.bfloat16),
            grad_ctx3,
            preferred_element_type=jnp.float32,
        )
        grad_pair = jnp.concatenate(
            [grad_keys.reshape(-1, model_dim), grad_vals.reshape(-1, model_dim)], axis=1
        )
        grad_ext = grad_ext.at[row_lo : row_lo + rows_group + block].add(grad_pair)
        returned = shifted(grad_ext[:block].astype(jnp.bfloat16), "fsdp", -1).astype(jnp.float32)
        grad_keyval = grad_ext[block:].at[tok_rows - block :].add(returned)
        local_memkv = jnp.concatenate(
            [
                grad_memkeys.reshape(basis_count, model_dim),
                grad_memvals.reshape(basis_count, model_dim),
            ],
            axis=1,
        )
        total_memkv = lax.psum(local_memkv.astype(jnp.bfloat16), "fsdp")
        own_count = basis_count // group_size
        own_coeffs = lax.dynamic_slice_in_dim(coeff_low, member * own_count, own_count)
        own_memkv = lax.dynamic_slice_in_dim(total_memkv, member * own_count, own_count)
        acc_qkv = acc_qkv.at[:, model_dim:].add(contract_rows(own_coeffs, own_memkv))
        grad_coeffs = contract_cols(total_memkv, full_qkv[:, model_dim:]).astype(jnp.bfloat16)
        grad_coeffs = lax.optimization_barrier(grad_coeffs).astype(jnp.float32)
        grad_fitted = jax.scipy.linalg.cho_solve((factor, True), grad_coeffs)
        grad_picked = jnp.dot(
            own_basis, grad_fitted, precision=HIGHEST, preferred_element_type=jnp.float32
        )
        grad_query = (query_parts + grad_query_mem).reshape(tok_rows, model_dim)
        grad_qkv = jnp.concatenate([grad_query, grad_keyval], axis=1).astype(jnp.bfloat16)
        acc_qkv = acc_qkv + contract_rows(first_low, grad_qkv)
        grad_first = contract_cols(grad_qkv, full_qkv).at[own_rows].add(grad_picked)
        grad_in_ln, gain_one_term, bias_one_term = norm_back(
            grad_first, normed_one, inv_one, gain_first
        )
        acc_gain_one = acc_gain_one + gain_one_term
        acc_bias_one = acc_bias_one + bias_one_term
        grads_list.append(grad_resid + grad_in_ln)
    vector_parts = [
        acc_gain_one,
        acc_bias_one,
        acc_gain_two,
        acc_bias_two,
        acc_hidden,
        acc_output,
        acc_mean,
        acc_spread,
    ]
    packed = jnp.concatenate([piece.reshape(group_size, -1) for piece in vector_parts], axis=1)
    packed = packed[:, None, :]
    split_qkv = acc_qkv.reshape(group_size, -1, acc_qkv.shape[1])
    split_out = acc_out.reshape(group_size, -1, acc_out.shape[1])
    split_fc = acc_fc.reshape(group_size, -1, acc_fc.shape[1])
    split_proj = acc_proj.reshape(group_size, -1, acc_proj.shape[1])
    part_qkv, part_out, part_fc, part_proj, part_vec = (
        lax.psum_scatter(
            split_qkv.astype(jnp.bfloat16), "rep", scatter_dimension=2, tiled=True
        ).astype(jnp.float32),
        lax.psum_scatter(
            split_out.astype(jnp.bfloat16), "rep", scatter_dimension=2, tiled=True
        ).astype(jnp.float32),
        lax.psum_scatter(
            split_fc.astype(jnp.bfloat16), "rep", scatter_dimension=2, tiled=True
        ).astype(jnp.float32),
        lax.psum_scatter(
            split_proj.astype(jnp.bfloat16), "rep", scatter_dimension=2, tiled=True
        ).astype(jnp.float32),
        lax.psum_scatter(
            packed.astype(jnp.bfloat16), "rep", scatter_dimension=2, tiled=True
        ).astype(jnp.float32),
    )
    own_qkv, own_out, own_fc, own_proj, own_vec = (
        lax.psum_scatter(
            part_qkv.astype(jnp.bfloat16), "fsdp", scatter_dimension=0, tiled=True
        ).astype(jnp.float32),
        lax.psum_scatter(
            part_out.astype(jnp.bfloat16), "fsdp", scatter_dimension=0, tiled=True
        ).astype(jnp.float32),
        lax.psum_scatter(
            part_fc.astype(jnp.bfloat16), "fsdp", scatter_dimension=0, tiled=True
        ).astype(jnp.float32),
        lax.psum_scatter(
            part_proj.astype(jnp.bfloat16), "fsdp", scatter_dimension=0, tiled=True
        ).astype(jnp.float32),
        lax.psum_scatter(
            part_vec.astype(jnp.bfloat16), "fsdp", scatter_dimension=0, tiled=True
        ).astype(jnp.float32),
    )
    sum_qkv, sum_out, sum_fc, sum_proj, sum_vec = (
        lax.all_gather(own_qkv.astype(jnp.bfloat16), "rep", axis=2, tiled=True).astype(
            own_qkv.dtype
        ),
        lax.all_gather(own_out.astype(jnp.bfloat16), "rep", axis=2, tiled=True).astype(
            own_out.dtype
        ),
        lax.all_gather(own_fc.astype(jnp.bfloat16), "rep", axis=2, tiled=True).astype(own_fc.dtype),
        lax.all_gather(own_proj.astype(jnp.bfloat16), "rep", axis=2, tiled=True).astype(
            own_proj.dtype
        ),
        lax.all_gather(own_vec.astype(jnp.bfloat16), "rep", axis=2, tiled=True).astype(
            own_vec.dtype
        ),
    )
    flat_vec = sum_vec[0, 0]
    model_share = model_dim // group_size
    hidden_share = hidden_dim // group_size
    basis_share = basis_count // group_size
    sizes_list = [
        model_share,
        model_share,
        model_share,
        model_share,
        hidden_share,
        model_share,
        basis_share * head_count,
        basis_share * head_count,
    ]
    pieces = []
    offset_now = 0
    for piece_len in sizes_list:
        pieces.append(flat_vec[offset_now : offset_now + piece_len])
        offset_now = offset_now + piece_len
    output_all = jnp.stack(outputs_list)[:, None]
    grad_tokens = jnp.stack(grads_list)[:, None]
    return (
        output_all,
        grad_tokens,
        sum_qkv[0],
        sum_out[0],
        sum_fc[0],
        sum_proj[0],
        pieces[0],
        pieces[1],
        pieces[2],
        pieces[3],
        pieces[4],
        pieces[5],
        pieces[6].reshape(basis_share, head_count),
        pieces[7].reshape(basis_share, head_count),
    )


def solution(mesh):
    return jax.shard_map(
        on_device,
        mesh=mesh,
        in_specs=(
            P(None, "rep", "fsdp", None),
            P(None, "rep", "fsdp", None),
            P(None, "rep", None),
            P(None, "rep", None),
            P("fsdp", None),
            P("fsdp", None),
            P("fsdp", None),
            P("fsdp", None),
            P("fsdp"),
            P("fsdp"),
            P("fsdp"),
            P("fsdp"),
            P("fsdp"),
            P("fsdp"),
            P("fsdp", None),
            P("fsdp", None),
        ),
        out_specs=(
            P(None, "rep", "fsdp", None),
            P(None, "rep", "fsdp", None),
            P("fsdp", None),
            P("fsdp", None),
            P("fsdp", None),
            P("fsdp", None),
            P("fsdp"),
            P("fsdp"),
            P("fsdp"),
            P("fsdp"),
            P("fsdp"),
            P("fsdp"),
            P("fsdp", None),
            P("fsdp", None),
        ),
        check_vma=False,
    )
```

profile of v0, /device:TPU:0, one launch (start us, length us, event | category | flops | bytes accessed | tf_op | source)
XLA Modules:
  0.0 1186.5 jit_solution(13166978022881725362)
XLA Ops:
  13.1 5.3 all-gather
  35.3 11.7 cholesky.130
  47.0 9.8 custom-call.17
  57.4 11.7 cholesky.147
  76.2 19.7 %custom-call.18 = f32[2,128,128]{1,2,0:T(8,128)S(1)} custom-call(f32[2,128,128]{2,1,0:T(8,128)S(1)} %get-tuple-element.139), custom_call_target="InvertDiagBlocksLowerTriangular" | custom-call | tf_op jit(solution)/shard_map/jit(_cho_solve)/triangular_solve | solution.py:199
  95.8 4.5 all_gather.54
  100.4 4.8 all_gather.55
  105.8 4.5 all-gather.2
  111.6 4.5 all-gather.3
  117.5 4.6 all-gather.4
  123.6 11.7 cholesky.164
  135.3 9.8 custom-call.19
  147.4 11.7 cholesky.181
  161.1 5.5 while.17
  166.7 20.3 %custom-call.20 = f32[2,128,128]{1,2,0:T(8,128)} custom-call(f32[2,128,128]{2,1,0:T(8,128)S(1)} %get-tuple-element.140), custom_call_target="InvertDiagBlocksLowerTriangular" | custom-call | tf_op jit(solution)/shard_map/jit(_cho_solve)/triangular_solve | solution.py:199
  243.2 4.6 collective-permute-start
  265.0 17.1 %collective-permute-done = bf16[256,1536]{1,0:T(8,128)(2,1)} collective-permute-done((bf16[256,1536]{1,0:T(8,128)(2,1)}, bf16[256,1536]{1,0:T(8,128)(2,1)}, u32[]{:S(2)}, u32[]{:S(2)}) %collective-permute-start) | collective-permute-done | bytes 786464 | tf_op jit(solution)/shard_map/ppermute | solution.py:21
  287.3 5.0 fusion
  292.3 4.5 exponential_reduce_fusion.1
  302.3 10.9 collective-permute-done.1
  318.7 9.5 fusion.1
  330.6 8.7 exponential_reduce_fusion
  339.4 9.8 add_convert_fusion.11
  353.3 8.9 add_convert_fusion.8
  364.8 8.3 fusion.342
  373.1 4.8 fusion.343
  377.9 11.2 convert_reduce_fusion.1
  389.1 7.6 convert_reduce_fusion
  410.9 4.8 fusion.356
  424.2 10.7 fusion.8
  441.8 17.1 %multiply_reduce_fusion = (f32[12,512]{1,0:T(8,128)S(1)}, f32[12,512,768]{2,1,0:T(8,128)}) fusion(f32[12,512,768]{2,1,0:T(8,128)} %get-tuple-element.321, f32[12,512]{1,0:T(8,128)S(1)} %log_add_fusion, pred[512,768]{1,0:T(8,128)(4,1)S(1)} %copy-done.23, bf16[512,12,64]{0,2,1:T(8,128)(2,1)S(1)} %bitcast.586, bf16[768,12,64]{0,2,1:T(8,128)(2,1)S(1)} %bitcast.591), kind=kOutput, calls=%fused_computation.9 | convolution fusion | flops 627566592 | bytes 40157184 | tf_op jit(solution)/shard_map/qhd,khd->hqk/dot_general | solution.py:296
  458.9 10.6 fusion.259
  471.5 9.5 multiply_convert_fusion
  494.1 17.2 %multiply_reduce_fusion.1 = (f32[12,512]{1,0:T(8,128)S(1)}, f32[12,512,768]{2,1,0:T(8,128)}) fusion(f32[12,512,768]{2,1,0:T(8,128)} %copy-done, f32[12,512]{1,0:T(8,128)S(1)} %copy-done.88, pred[512,768]{1,0:T(8,128)(4,1)S(1)} %copy-done.22, bf16[512,12,64]{0,2,1:T(8,128)(2,1)S(1)} %bitcast.600, bf16[768,12,64]{0,2,1:T(8,128)(2,1)S(1)} %bitcast.589), kind=kOutput, calls=%fused_computation.11 | convolution fusion | flops 627566592 | bytes 40157184 | tf_op jit(solution)/shard_map/qhd,khd->hqk/dot_general | solution.py:296
  511.4 10.4 fusion.262
  521.8 6.0 fusion.341
  530.1 10.1 fusion.188
  540.2 8.4 multiply_convert_fusion.10
  550.0 9.5 multiply_convert_fusion.1
  564.9 9.2 multiply_convert_fusion.11
  576.6 6.9 add_convert_fusion.1
  583.5 11.7 add_convert_fusion
  602.2 12.5 %copy.156 = bf16[2,384,3072]{1,0,2:T(2,128)(2,1)} copy(bf16[2,384,3072]{2,1,0:T(8,128)(2,1)} %bitcast.592) | data formatting | bytes 9437184 | tf_op jit(solution)/shard_map/convert_element_type | solution.py:373
  617.5 12.5 %copy.158 = bf16[2,1536,768]{1,0,2:T(2,128)(2,1)} copy(bf16[2,1536,768]{2,1,0:T(8,128)(2,1)} %bitcast.593) | data formatting | bytes 9437184 | tf_op jit(solution)/shard_map/convert_element_type | solution.py:376
  633.0 6.6 fusion.143
  641.9 11.1 all-reduce.21.cloned.1.call-done
  652.9 5.6 constant_dynamic-update-slice_fusion.10
  661.6 5.6 add_convert_fusion.2
  667.2 7.1 copy.152
  678.8 4.6 all-gather.5
  684.7 7.9 fusion.44
  692.7 8.0 fusion.36
  700.7 8.3 fusion.151
  709.0 221.7 %all-reduce.19.cloned.1.call-done = (bf16[2,384,2304]{1,0,2:T(2,128)(2,1)}, bf16[2,384,768]{1,0,2:T(2,128)(2,1)}, bf16[2,384,3072]{1,0,2:T(2,128)(2,1)}, bf16[2,1536,768]{1,0,2:T(2,128)(2,1)}) async-done(((bf16[2,384,2304]{1,0,2:T(2,128)(2,1)}, bf16[2,384,768]{1,0,2:T(2,128)(2,1)}, bf16[2,384,3072]{1,0,2:T(2,128)(2,1)}, bf16[2,1536,768]{1,0,2:T(2,128)(2,1)}), (bf16[2,384,2304]{1,0,2:T(2,128)(2,1)}, ...) | async-done | bytes 14155792
  933.0 7.8 fusion.46
  942.9 8.0 fusion.38
  959.3 8.3 fusion.152
  1001.1 60.3 %all-reduce.8 = bf16[2,1,6528]{2,0,1:T(2,128)(2,1)S(1)} all-reduce(bf16[2,1,6528]{2,0,1:T(2,128)(2,1)S(1)} %constant_dynamic-update-slice_fusion), channel_id=10, replica_groups=mesh['rep'=16,'fsdp'=2] {'rep'}, use_global_device_ids=true, to_apply=%region_58.63.clone | all-reduce | flops 13056 | bytes 52224
  1061.5 4.9 all-reduce.9
  1067.3 58.4 %all-reduce.3 = bf16[6528]{0:T(1024)(128)(2,1)S(1)} all-reduce(bf16[6528]{0:T(1024)(128)(2,1)S(1)} %dynamic-update-slice.28), channel_id=1, replica_groups=mesh['rep'=16,'fsdp'=2] {'rep'}, use_global_device_ids=true, to_apply=%add.3 | all-reduce | flops 6528 | bytes 26112
  1133.4 19.4 %all_gather.64 = bf16[1,384,768]{1,2,0:T(8,128)(2,1)S(1)} all-gather(bf16[1,384,48]{1,2,0:T(8,128)(2,1)} %reduce-scatter.9.cloned.1.call-done), channel_id=1, replica_groups=mesh['rep'=16,'fsdp'=2] {'rep'}, dimensions={2}, use_global_device_ids=true | all-gather | bytes 626688 | tf_op jit(solution)/shard_map/all_gather | solution.py:403
  1163.1 6.0 copy.164
  1169.2 4.5 bitcast_convert_fusion
  1173.7 6.0 copy.165
  (694 shorter events, 284.4 us)
Async XLA Ops:
  7.2 16.4 %copy-start.8 = (bf16[2,1,512,768]{3,2,1,0:T(8,128)(2,1)S(1)}, bf16[2,1,512,768]{3,2,1,0:T(8,128)(2,1)}, u32[]{:S(2)}) copy-start(bf16[2,1,512,768]{3,2,1,0:T(8,128)(2,1)} %param.38) | copy-start | bytes 4718596
  7.2 184.7 %all-reduce.17.cloned.1.call-start = ((), (), s32[]{:S(2)}) async-start(), calls=%async_computation.15 | async-start | bytes 3145728 | tf_op jit(solution)/shard_map/psum | solution.py:198
  7.3 26.7 %copy-start.162 = (f32[256]{0:T(256)}, f32[256]{0:T(256)S(1)}, u32[]{:S(2)}) copy-start(f32[256]{0:T(256)S(1)} %add_multiply_fusion) | copy-start | bytes 3076
  8.7 14.9 %copy-start.150 = (s32[1,1,128]{2,1,0:T(1,128)}, s32[1,1,128]{2,1,0:T(1,128)S(1)}, u32[]{:S(2)}) copy-start(s32[1,1,128]{2,1,0:T(1,128)S(1)} %get-tuple-element.314) | copy-start | bytes 1540
  8.7 14.9 %copy-start.152 = (s32[1,1,128]{2,1,0:T(1,128)}, s32[1,1,128]{2,1,0:T(1,128)S(1)}, u32[]{:S(2)}) copy-start(s32[1,1,128]{2,1,0:T(1,128)S(1)} %get-tuple-element.315) | copy-start | bytes 1540
  10.4 14.6 %copy-start.108 = (f32[512]{0:T(512)}, f32[512]{0:T(512)S(1)}, u32[]{:S(2)}) copy-start(f32[512]{0:T(512)S(1)} %get-tuple-element.341) | copy-start | bytes 6148
  10.4 14.6 %copy-start.110 = (f32[512]{0:T(512)}, f32[512]{0:T(512)S(1)}, u32[]{:S(2)}) copy-start(f32[512]{0:T(512)S(1)} %get-tuple-element.342) | copy-start | bytes 6148
  12.4 12.6 %copy-start.112 = (f32[512]{0:T(512)}, f32[512]{0:T(512)S(1)}, u32[]{:S(2)}) copy-start(f32[512]{0:T(512)S(1)} %add_rsqrt_fusion.1) | copy-start | bytes 6148
  12.4 12.6 %copy-start.114 = (f32[512]{0:T(512)}, f32[512]{0:T(512)S(1)}, u32[]{:S(2)}) copy-start(f32[512]{0:T(512)S(1)} %add_rsqrt_fusion.3) | copy-start | bytes 6148
  24.3 180.1 %copy-start.24 = (bf16[512,768]{1,0:T(8,128)(2,1)}, bf16[512,768]{1,0:T(8,128)(2,1)S(1)}, u32[]{:S(2)}) copy-start(bf16[512,768]{1,0:T(8,128)(2,1)S(1)} %get-tuple-element.277) | copy-start | bytes 2359300
  29.4 174.9 %all-gather.14.cloned.1.call-start = ((), (), s32[]{:S(2)}) async-start(), calls=%async_computation.4 | async-start | bytes 5308416 | tf_op jit(solution)/shard_map/all_gather | solution.py:121
  30.2 319.1 %all-gather.16.cloned.1.call-start = ((), (), s32[]{:S(2)}) async-start(), calls=%async_computation.5 | async-start | bytes 1769472 | tf_op jit(solution)/shard_map/all_gather | solution.py:122
  30.9 333.8 %all-gather.18.cloned.1.call-start = ((), (), s32[]{:S(2)}) async-start(), calls=%async_computation.6 | async-start | bytes 7077888 | tf_op jit(solution)/shard_map/all_gather | solution.py:123
  31.5 64.4 %copy-start.154 = (bf16[128,12]{0,1:T(8,128)(2,1)S(1)}, bf16[128,12]{0,1:T(8,128)(2,1)}, u32[]{:S(2)}) copy-start(bf16[128,12]{0,1:T(8,128)(2,1)} %param.53) | copy-start | bytes 9220
  31.5 346.4 %all-gather.20.cloned.1.call-start = ((), (), s32[]{:S(2)}) async-start(), calls=%async_computation.7 | async-start | bytes 7077888 | tf_op jit(solution)/shard_map/all_gather | solution.py:124
  32.1 620.9 %all-reduce.21.cloned.1.call-start = ((), (), s32[]{:S(2)}) async-start(), calls=%async_computation.17 | async-start | bytes 3145728 | tf_op jit(solution)/shard_map/psum | solution.py:328
  76.2 119.0 %copy-start.51 = (f32[256,256]{1,0:T(8,128)}, f32[256,256]{1,0:T(8,128)S(1)}, u32[]{:S(2)}) copy-start(f32[256,256]{1,0:T(8,128)S(1)} %get-tuple-element.483) | copy-start | bytes 786436
  95.8 99.3 %copy-start.55 = (f32[2,128,128]{1,2,0:T(8,128)}, f32[2,128,128]{1,2,0:T(8,128)S(1)}, u32[]{:S(2)}) copy-start(f32[2,128,128]{1,2,0:T(8,128)S(1)} %custom-call.18) | copy-start | bytes 393220
  166.7 25.3 %copy-start.53 = (f32[256,256]{1,0:T(8,128)}, f32[256,256]{1,0:T(8,128)S(1)}, u32[]{:S(2)}) copy-start(f32[256,256]{1,0:T(8,128)S(1)} %get-tuple-element.484) | copy-start | bytes 786436
  191.9 147.5 %copy-start.21 = (pred[512,768]{1,0:T(8,128)(4,1)}, pred[512,768]{1,0:T(8,128)(4,1)S(1)}, u32[]{:S(2)}) copy-start(pred[512,768]{1,0:T(8,128)(4,1)S(1)} %get-tuple-element.302) | copy-start | bytes 1179652
  217.2 70.1 %copy-start.14 = (bf16[512,768]{0,1:T(8,128)(2,1)}, bf16[512,768]{0,1:T(8,128)(2,1)S(1)}, u32[]{:S(2)}) copy-start(bf16[512,768]{0,1:T(8,128)(2,1)S(1)} %copy.133) | copy-start | bytes 2359300
  240.4 17.6 %copy-start.163 = (f32[256]{0:T(256)S(1)}, f32[256]{0:T(256)}, u32[]{:S(2)}) copy-start(f32[256]{0:T(256)} %copy-done.162) | copy-start | bytes 3076
  243.2 38.9 %collective-permute-start = (bf16[256,1536]{1,0:T(8,128)(2,1)}, bf16[256,1536]{1,0:T(8,128)(2,1)}, u32[]{:S(2)}, u32[]{:S(2)}) collective-permute-start(bf16[256,1536]{1,0:T(8,128)(2,1)} %slice.347), channel_id=1, source_target_pairs={{0,1},{2,3},{4,5},{6,7},{8,9},{10,11},{12,13},{14,15},{16,17},{18,... | collective-permute-start | bytes 2359304 | tf_op jit(solution)/shard_map/ppermute | solution.py:21
  251.1 62.1 %collective-permute-start.1 = (bf16[256,1536]{1,0:T(8,128)(2,1)}, bf16[256,1536]{1,0:T(8,128)(2,1)}, u32[]{:S(2)}, u32[]{:S(2)}) collective-permute-start(bf16[256,1536]{1,0:T(8,128)(2,1)} %slice.355), channel_id=1, source_target_pairs={{0,1},{2,3},{4,5},{6,7},{8,9},{10,11},{12,13},{14,15},{16,17},{18,... | collective-permute-start | bytes 2359304 | tf_op jit(solution)/shard_map/ppermute | solution.py:21
  262.0 20.1 %slice-start.5 = ((bf16[512,2304]{1,0:T(8,128)(2,1)}), bf16[512,1536]{1,0:T(8,128)(2,1)S(1)}, s32[]{:S(2)}) async-start(bf16[512,2304]{1,0:T(8,128)(2,1)} %copy-done.29), calls=%async_computation.23 | async-start | bytes 3145728 | tf_op jit(solution)/shard_map/slice | solution.py:180
  302.3 37.1 %copy-start.87 = (f32[12,512]{1,0:T(8,128)}, f32[12,512]{1,0:T(8,128)S(1)}, u32[]{:S(2)}) copy-start(f32[12,512]{1,0:T(8,128)S(1)} %log_add_fusion.1) | copy-start | bytes 73732
  302.3 16.4 %copy-start.23 = (pred[512,768]{1,0:T(8,128)(4,1)S(1)}, pred[512,768]{1,0:T(8,128)(4,1)}, u32[]{:S(2)}) copy-start(pred[512,768]{1,0:T(8,128)(4,1)} %get-tuple-element.303) | copy-start | bytes 1179652
  363.2 40.2 %copy-start.130 = (f32[512]{0:T(512)}, f32[512]{0:T(512)S(1)}, u32[]{:S(2)}) copy-start(f32[512]{0:T(512)S(1)} %broadcast_multiply_fusion.8) | copy-start | bytes 6148
  364.7 38.7 %copy-start.144 = (f32[512]{0:T(512)}, f32[512]{0:T(512)S(1)}, u32[]{:S(2)}) copy-start(f32[512]{0:T(512)S(1)} %add_rsqrt_fusion) | copy-start | bytes 6148
  377.9 18.8 %slice-start.7 = ((s8[4718592]{0:T(1024)(128)(4,1)}), s8[4194304]{0:T(1024)(128)(4,1)S(1)}, s32[]{:S(2)}) async-start(s8[4718592]{0:T(1024)(128)(4,1)} %bitcast.642), calls=%async_computation.25 | async-start | bytes 8388608
  405.7 12.7 %copy-start.18 = (f32[512,768]{1,0:T(8,128)}, f32[512,768]{1,0:T(8,128)S(1)}, u32[]{:S(2)}) copy-start(f32[512,768]{1,0:T(8,128)S(1)} %get-tuple-element.283) | copy-start | bytes 4718596
  458.9 12.6 %copy-start.5 = (f32[12,512,768]{2,1,0:T(8,128)S(1)}, f32[12,512,768]{2,1,0:T(8,128)}, u32[]{:S(2)}) copy-start(f32[12,512,768]{2,1,0:T(8,128)} %get-tuple-element.334) | copy-start | bytes 56623108
  530.0 19.9 %slice-start = ((s8[18874368]{0:T(1024)(128)(4,1)}), s8[4194304]{0:T(1024)(128)(4,1)S(1)}, s32[]{:S(2)}) async-start(s8[18874368]{0:T(1024)(128)(4,1)} %bitcast.558), calls=%async_computation.18 | async-start | bytes 8388608
  530.0 19.9 %slice-start.1 = ((s8[18874368]{0:T(1024)(128)(4,1)}), s8[4194304]{0:T(1024)(128)(4,1)S(1)}, s32[]{:S(2)}) async-start(s8[18874368]{0:T(1024)(128)(4,1)} %bitcast.558), calls=%async_computation.19 | async-start | bytes 8388608
  530.0 19.9 %slice-start.2 = ((s8[18874368]{0:T(1024)(128)(4,1)}), s8[4194304]{0:T(1024)(128)(4,1)S(1)}, s32[]{:S(2)}) async-start(s8[18874368]{0:T(1024)(128)(4,1)} %bitcast.558), calls=%async_computation.20 | async-start | bytes 8388608
  530.0 19.9 %slice-start.3 = ((s8[18874368]{0:T(1024)(128)(4,1)}), s8[4194304]{0:T(1024)(128)(4,1)S(1)}, s32[]{:S(2)}) async-start(s8[18874368]{0:T(1024)(128)(4,1)} %bitcast.558), calls=%async_computation.21 | async-start | bytes 8388608
  548.6 90.9 %collective-permute-start.3 = (bf16[256,1536]{0,1:T(8,128)(2,1)}, bf16[256,1536]{0,1:T(8,128)(2,1)}, u32[]{:S(2)}, u32[]{:S(2)}) collective-permute-start(bf16[256,1536]{0,1:T(8,128)(2,1)} %fusion.140), channel_id=1, source_target_pairs={{1,0},{3,2},{5,4},{7,6},{9,8},{11,10},{13,12},{15,14},{17,16},{19,... | collective-permute-start | bytes 2359304 | tf_op jit(solution)/shard_map/ppermute | solution.py:21
  563.2 13.3 %slice-start.9 = ((s8[9437184]{0:T(1024)(128)(4,1)}), s8[4194304]{0:T(1024)(128)(4,1)S(1)}, s32[]{:S(2)}) async-start(s8[9437184]{0:T(1024)(128)(4,1)} %bitcast.644), calls=%async_computation.27 | async-start | bytes 8388608
  563.2 13.3 %slice-start.10 = ((s8[9437184]{0:T(1024)(128)(4,1)}), s8[4194304]{0:T(1024)(128)(4,1)S(1)}, s32[]{:S(2)}) async-start(s8[9437184]{0:T(1024)(128)(4,1)} %bitcast.644), calls=%async_computation.28 | async-start | bytes 8388608
  575.1 55.0 %collective-permute-start.2 = (bf16[256,1536]{0,1:T(8,128)(2,1)}, bf16[256,1536]{0,1:T(8,128)(2,1)}, u32[]{:S(2)}, u32[]{:S(2)}) collective-permute-start(bf16[256,1536]{0,1:T(8,128)(2,1)} %fusion.141), channel_id=1, source_target_pairs={{1,0},{3,2},{5,4},{7,6},{9,8},{11,10},{13,12},{15,14},{17,16},{19,... | collective-permute-start | bytes 2359304 | tf_op jit(solution)/shard_map/ppermute | solution.py:21
  583.4 11.7 copy-start.84
  583.4 12.7 %copy-start.83 = (bf16[12,64,256]{2,1,0:T(8,128)(2,1)S(1)}, bf16[12,64,256]{2,1,0:T(8,128)(2,1)}, u32[]{:S(2)}) copy-start(bf16[12,64,256]{2,1,0:T(8,128)(2,1)} %fusion.160) | copy-start | bytes 1179652
  583.5 12.7 %copy-start.85 = (bf16[12,64,256]{2,1,0:T(8,128)(2,1)S(1)}, bf16[12,64,256]{2,1,0:T(8,128)(2,1)}, u32[]{:S(2)}) copy-start(bf16[12,64,256]{2,1,0:T(8,128)(2,1)} %fusion.167) | copy-start | bytes 1179652
  597.1 333.6 %all-reduce.19.cloned.1.call-start = ((), (), s32[]{:S(2)}) async-start(), calls=%async_computation.16 | async-start | bytes 28311552
  639.6 13.4 %copy-start.69 = (bf16[256,768]{1,0:T(8,128)(2,1)S(1)}, bf16[256,768]{1,0:T(8,128)(2,1)}, u32[]{:S(2)}) copy-start(bf16[256,768]{1,0:T(8,128)(2,1)} %maximum_convert_fusion) | copy-start | bytes 1179652
  674.4 18.2 %copy-start.103 = (f32[512,12]{0,1:T(8,128)S(1)}, f32[512,12]{0,1:T(8,128)}, u32[]{:S(2)}) copy-start(f32[512,12]{0,1:T(8,128)} %copy-done.102) | copy-start | bytes 73732
  674.4 283.9 %reduce-scatter.7.cloned.1.call-start = ((), (), s32[]{:S(2)}) async-start(), calls=%async_computation.8 | async-start | bytes 331776 | tf_op jit(solution)/shard_map/reduce_scatter | solution.py:383
  700.7 232.3 %copy-start.101 = (f32[12,512]{1,0:T(8,128)S(1)}, f32[12,512]{1,0:T(8,128)}, u32[]{:S(2)}) copy-start(f32[12,512]{1,0:T(8,128)} %copy-done.100) | copy-start | bytes 73732
  932.5 45.9 %reduce-scatter.11.cloned.1.call-start = ((), (), s32[]{:S(2)}) async-start(), calls=%async_computation.11 | async-start | bytes 442368 | tf_op jit(solution)/shard_map/reduce_scatter | solution.py:389
  942.8 58.2 %reduce-scatter.13.cloned.1.call-start = ((), (), s32[]{:S(2)}) async-start(), calls=%async_computation.13 | async-start | bytes 442368 | tf_op jit(solution)/shard_map/reduce_scatter | solution.py:392
  942.8 12.0 %copy-start.159 = (f32[768]{0:T(1024)S(1)}, f32[768]{0:T(1024)}, u32[]{:S(2)}) copy-start(f32[768]{0:T(1024)} %get-tuple-element.207) | copy-start | bytes 9220
  942.9 12.0 %copy-start.160 = (f32[768]{0:T(1024)S(1)}, f32[768]{0:T(1024)}, u32[]{:S(2)}) copy-start(f32[768]{0:T(1024)} %get-tuple-element.309) | copy-start | bytes 9220
  942.9 12.6 %copy-start.157 = (f32[768]{0:T(1024)S(1)}, f32[768]{0:T(1024)}, u32[]{:S(2)}) copy-start(f32[768]{0:T(1024)} %get-tuple-element.223) | copy-start | bytes 9220
  942.9 12.6 %copy-start.158 = (f32[768]{0:T(1024)S(1)}, f32[768]{0:T(1024)}, u32[]{:S(2)}) copy-start(f32[768]{0:T(1024)} %get-tuple-element.306) | copy-start | bytes 9220
  942.9 14.8 %copy-start.142 = (f32[3072]{0:T(1024)S(1)}, f32[3072]{0:T(1024)}, u32[]{:S(2)}) copy-start(f32[3072]{0:T(1024)} %get-tuple-element.337) | copy-start | bytes 36868
  942.9 14.8 %copy-start.143 = (f32[3072]{0:T(1024)S(1)}, f32[3072]{0:T(1024)}, u32[]{:S(2)}) copy-start(f32[3072]{0:T(1024)} %get-tuple-element.339) | copy-start | bytes 36868
  942.9 15.7 %copy-start.133 = (f32[768]{0:T(1024)S(1)}, f32[768]{0:T(1024)}, u32[]{:S(2)}) copy-start(f32[768]{0:T(1024)} %get-tuple-element.220) | copy-start | bytes 9220
  942.9 15.7 %copy-start.134 = (f32[768]{0:T(1024)S(1)}, f32[768]{0:T(1024)}, u32[]{:S(2)}) copy-start(f32[768]{0:T(1024)} %get-tuple-element.221) | copy-start | bytes 9220
  942.9 16.3 %copy-start.34 = (f32[512,768]{1,0:T(8,128)S(1)}, f32[512,768]{1,0:T(8,128)}, u32[]{:S(2)}) copy-start(f32[512,768]{1,0:T(8,128)} %copy-done.30) | copy-start | bytes 4718596
  953.3 180.1 %reduce-scatter.9.cloned.1.call-start = ((), (), s32[]{:S(2)}) async-start(), calls=%async_computation.10 | async-start | bytes 110592 | tf_op jit(solution)/shard_map/reduce_scatter | solution.py:386
  957.7 196.6 %all-gather.22.cloned.1.call-start = ((), (), s32[]{:S(2)}) async-start(), calls=%async_computation.9 | async-start | bytes 1880064 | tf_op jit(solution)/shard_map/all_gather | solution.py:400
  958.4 200.6 %all-gather.24.cloned.1.call-start = ((), (), s32[]{:S(2)}) async-start(), calls=%async_computation.12 | async-start | bytes 2506752 | tf_op jit(solution)/shard_map/all_gather | solution.py:406
  978.4 190.7 %all-gather.26.cloned.1.call-start = ((), (), s32[]{:S(2)}) async-start(), calls=%async_computation.14 | async-start | bytes 2506752 | tf_op jit(solution)/shard_map/all_gather | solution.py:407
  998.1 130.5 %copy-start.115 = (f32[512]{0:T(512)S(1)}, f32[512]{0:T(512)}, u32[]{:S(2)}) copy-start(f32[512]{0:T(512)} %copy-done.114) | copy-start | bytes 6148
  (146 other events, 745.9 us)
Sparse Core Ops, SparseCore 0:
  29.5 53.4 all-reduce.16
  84.6 49.7 all-gather.13
  136.0 22.7 all-gather.15
  160.2 62.7 all-gather.17
  224.3 94.1 all-gather.19
  597.2 55.6 all-reduce.20
  674.5 256.1 all-reduce.18
  933.5 11.3 reduce-scatter.6
  947.7 12.1 reduce-scatter.10
  962.5 12.1 reduce-scatter.12
  977.5 10.0 reduce-scatter.8
  989.6 40.5 all-gather.21
  1032.5 41.1 all-gather.23
  1075.8 41.2 all-gather.25
where the time goes:
time: 1190 us
  matrix products  371 us (31%)
  waiting for transfers between devices  263 us (22%)
  other arithmetic  203 us (17%)
  blocking collectives  180 us (15%)
  local copies, waits for them, and re-layouts  134 us (11%)
  between operations  22.9 us (2%)
    unnamed x15, waiting for transfers between devices  224 us
    unnamed x3, blocking collectives  124 us
    another operation x12, other arithmetic, on_device(): factor = jnp.linalg.cholesky(system)  67.9 us
    dot_general x10, matrix products, contract_rows(): lax.dot_general(first_op, second_op, (((0,), (0,)), ((), ())), preferred_...  61 us
    unnamed x409, local copies, waits for them, and re-layouts  48.6 us
    another operation x5, other arithmetic, on_device(): coeffs = jax.scipy.linalg.cho_solve((factor, True), fitted)  40 us
    dot_general x10, matrix products, contract_cols(): lax.dot_general(first_op, second_op, (((1,), (1,)), ((), ())), preferred_...  36.9 us
    dot_general x2, matrix products, on_device(): jnp.einsum('qhd,khd->hqk', grad_ctx3, val_part, preferred_element_type=jn...  34.3 us
  transfers between devices with their start and end apart: 18, of which 4 were waited for; matrix products, arithmetic and copies ran while one was open for 40% of the time, Pallas kernels for 0%

commit v1 on v0

v1 whole, which is shorter than its diff:
```python
from functools import partial

import jax
import jax.numpy as jnp
from jax import lax
from jax.experimental import pallas as pl
from jax.experimental.pallas import tpu as pltpu
from jax.sharding import PartitionSpec as P

BLK = 256
CHUNK = 512
TILE = 256
HIGHEST = lax.Precision.HIGHEST
EPSILON = 1e-05
RIDGE_TERM = 0.5
SIGMA_SCALE = 0.01
MASKED = -1e30
F32 = jnp.float32
BF16 = jnp.bfloat16
VMEM_BYTES = 60 * 1024 * 1024


def dot(a, b, ca=1, cb=0):
    return lax.dot_general(a, b, (((ca,), (cb,)), ((), ())), preferred_element_type=F32)


def row_spec(shape, index):
    return pl.BlockSpec(shape, index)


def params(limit=VMEM_BYTES):
    return pltpu.CompilerParams(vmem_limit_bytes=limit)


def layer_norm(inputs, gains, offsets):
    centred = inputs - jnp.mean(inputs, axis=-1, keepdims=True)
    inv_std = lax.rsqrt(jnp.mean(centred * centred, axis=-1, keepdims=True) + EPSILON)
    normed = centred * inv_std
    return (normed * gains + offsets, normed, inv_std)


def basis_rows(sample_pos, length, basis_count):
    times = (sample_pos.astype(F32) + 0.5) / length
    centres = (jnp.arange(basis_count, dtype=F32) + 0.5) / basis_count
    width = 1.25 / basis_count
    return jnp.exp(-((times[..., None] - centres) ** 2) / (2.0 * width * width))


def inverse_kernel(a_ref, o_ref):
    count, size = a_ref.shape[0], a_ref.shape[1]
    lanes = lax.broadcasted_iota(jnp.int32, (1, size), 1)
    rows = lax.broadcasted_iota(jnp.int32, (size, 1), 0)
    for m in range(count):
        o_ref[m] = a_ref[m]

    def eliminate(k, carry):
        here = lanes == k
        for m in range(count):
            full = o_ref[m]
            row = o_ref[m, pl.ds(k, 1), :]
            pivot = jnp.sum(jnp.where(here, row, 0.0), axis=1, keepdims=True)
            column = jnp.sum(jnp.where(here, full, 0.0), axis=1, keepdims=True)
            recip = 1.0 / pivot
            scaled = jnp.where(here, recip, row * recip)
            kept = jnp.where(here, 0.0, full)
            o_ref[m] = jnp.where(rows == k, scaled, kept - column * scaled)
        return carry

    lax.fori_loop(0, size, eliminate, 0)


def spd_inverse(systems):
    return pl.pallas_call(
        inverse_kernel,
        out_shape=jax.ShapeDtypeStruct(systems.shape, F32),
        compiler_params=params(),
        cost_estimate=pl.CostEstimate(flops=20_000_000, bytes_accessed=300_000, transcendentals=0),
        name="inverse",
    )(systems)


def pick(stats, lanes, index):
    return jnp.sum(jnp.where(lanes == index, stats, 0.0), axis=1, keepdims=True)


def forward_kernel(q_ref, k_ref, v_ref, dcol_ref, drow_ref, st_ref, c_ref, p_ref, e_ref, *, ext):
    pair = pl.program_id(1)
    basis = k_ref.shape[1] - ext
    lanes = lax.broadcasted_iota(jnp.int32, (1, 128), 1)
    centres = (lax.broadcasted_iota(jnp.int32, (1, basis), 1).astype(F32) + 0.5) / basis
    mem_v = v_ref[0, ext:, :]
    for i in range(ext // BLK - 1):
        lo = i * BLK
        queries = q_ref[0, lo : lo + BLK, :] * BF16(0.125)
        keys = k_ref[0, lo : lo + 2 * BLK, :]
        vals = v_ref[0, lo : lo + 2 * BLK, :]
        allowed = dcol_ref[0, lo + BLK : lo + 2 * BLK, :] == drow_ref[0, :, lo : lo + 2 * BLK]
        stats = st_ref[0, lo : lo + BLK, :]
        mixed = []
        for half in range(2):
            head = 2 * pair + half
            mine = (lanes // 64) == half
            scores = dot(jnp.where(mine, queries, BF16(0)), keys, 1, 1)
            scores = jnp.where(allowed, scores, MASKED)
            top = jnp.max(scores, axis=1, keepdims=True)
            probs = jnp.exp(scores - top)
            probs = probs * (1.0 / jnp.sum(probs, axis=1, keepdims=True))
            probs = probs.astype(BF16)
            p_ref[0, half, i] = probs
            gap = pick(stats, lanes, head) - centres
            density = pick(stats, lanes, 32 + head) * jnp.exp(
                -(gap * gap) * pick(stats, lanes, 16 + head)
            )
            density = density.astype(BF16)
            e_ref[0, half, lo : lo + BLK, :] = density
            mixed.append(dot(probs, vals) + dot(density, mem_v))
        c_ref[0, lo : lo + BLK, :] = jnp.where(lanes < 64, mixed[0], mixed[1]).astype(BF16)


def backward_kernel(
    dc_ref, q_ref, k_ref, v_ref, p_ref, e_ref, st_ref, km_ref, ks_ref, mw_ref, sw_ref,
    dq_ref, dk_ref, dv_ref, qm_ref, dk_acc, dv_acc, *, ext
):
    pair = pl.program_id(1)
    basis = k_ref.shape[1] - ext
    lanes = lax.broadcasted_iota(jnp.int32, (1, 128), 1)
    centres = (lax.broadcasted_iota(jnp.int32, (1, basis), 1).astype(F32) + 0.5) / basis
    mem_v = v_ref[0, ext:, :]
    dk_acc[...] = jnp.zeros_like(dk_acc)
    dv_acc[...] = jnp.zeros_like(dv_acc)
    km, ks = km_ref[0], ks_ref[0]
    sum_m = jnp.zeros((1, 128), F32)
    sum_s = jnp.zeros((1, 128), F32)
    for i in range(ext // BLK - 1):
        lo = i * BLK
        raw = q_ref[0, lo : lo + BLK, :]
        queries = raw * BF16(0.125)
        keys = k_ref[0, lo : lo + 2 * BLK, :]
        vals = v_ref[0, lo : lo + 2 * BLK, :]
        grads = dc_ref[0, lo : lo + BLK, :]
        stats = st_ref[0, lo : lo + BLK, :]
        dq_parts, dm_parts, dsp_parts = [], [], []
        for half in range(2):
            head = 2 * pair + half
            mine = (lanes // 64) == half
            own_grad = jnp.where(mine, grads, BF16(0))
            own_q = jnp.where(mine, queries, BF16(0))
            probs = p_ref[0, half, i]
            wide = probs.astype(F32)
            prod = wide * dot(own_grad, vals, 1, 1)
            total = jnp.sum(prod, axis=1, keepdims=True)
            dscore = (prod - wide * total).astype(BF16)
            dq_parts.append(dot(dscore, keys))
            dk_acc[lo : lo + 2 * BLK, :] += dot(dscore, own_q, 0, 0)
            dv_acc[lo : lo + 2 * BLK, :] += dot(probs, own_grad, 0, 0)
            density = e_ref[0, half, lo : lo + BLK, :]
            dv_acc[ext:, :] += dot(density, own_grad, 0, 0)
            weight = density.astype(F32) * dot(own_grad, mem_v, 1, 1)
            gap = pick(stats, lanes, head) - centres
            first = weight * gap
            s_zero = jnp.sum(weight, axis=1, keepdims=True)
            s_one = jnp.sum(first, axis=1, keepdims=True)
            s_two = jnp.sum(first * gap, axis=1, keepdims=True)
            dm_parts.append(s_one * pick(stats, lanes, 48 + head))
            dsp_parts.append(
                s_two * pick(stats, lanes, 64 + head) + s_zero * pick(stats, lanes, 80 + head)
            )
        low = lanes < 64
        d_mean = jnp.where(low, dm_parts[0], dm_parts[1])
        d_spread = jnp.where(low, dsp_parts[0], dsp_parts[1])
        dq = jnp.where(low, dq_parts[0], dq_parts[1]) * 0.125 + d_mean * km + d_spread * ks
        dq_ref[0, lo : lo + BLK, :] = dq.astype(BF16)
        wide_q = raw.astype(F32)
        sum_m += jnp.sum(d_mean * wide_q, axis=0, keepdims=True)
        sum_s += jnp.sum(d_spread * wide_q, axis=0, keepdims=True)
    dk_ref[0, :ext, :] = dk_acc[:ext, :].astype(BF16)
    dk_ref[0, ext:, :] = (0.125 * (mw_ref[...] * sum_m + sw_ref[...] * sum_s)).astype(BF16)
    dv_ref[0] = dv_acc[...].astype(BF16)
    rows = lax.broadcasted_iota(jnp.int32, (8, 1), 0)
    qm_ref[0] = jnp.where(rows == 0, sum_m, jnp.where(rows == 1, sum_s, 0.0))


def middle_kernel(
    x_ref, cot_ref, c_ref, wout_ref, wfc_ref, wproj_ref, vec_ref, fcb_ref,
    out_ref, dr_ref, dc_ref, dwout_ref, dwfc_ref, dwproj_ref, dfcb_ref, vecg_ref,
    r_s, h_s, y_s, g_s, act_s, du_s, do_s
):
    chunk = pl.program_id(0)
    tiles = x_ref.shape[0] // TILE
    gain, bias, out_bias = vec_ref[0:1, :], vec_ref[1:2, :], vec_ref[2:3, :]

    def rows_of(t):
        return pl.ds(pl.multiple_of(t * TILE, TILE), TILE)

    @pl.when(chunk == 0)
    def _():
        def start(t, carry):
            rows = rows_of(t)
            resid = x_ref[rows, :].astype(F32) + dot(c_ref[rows, :], wout_ref[...])
            r_s[rows, :] = resid
            h_s[rows, :] = layer_norm(resid, gain, bias)[0].astype(BF16)
            y_s[rows, :] = resid + out_bias
            g_s[rows, :] = jnp.zeros((TILE, g_s.shape[1]), F32)
            return carry

        lax.fori_loop(0, tiles, start, 0)

    wfc, wproj, fcb = wfc_ref[...], wproj_ref[...], fcb_ref[0]

    def body(t, sums):
        rows = rows_of(t)
        pre = dot(h_s[rows, :], wfc) + fcb
        sq = pre * pre
        th = jnp.tanh(pre * (0.7978845608028654 + 0.035677408136300125 * sq))
        half = 0.5 * (1.0 + th)
        act = (pre * half).astype(BF16)
        slope = half + 0.5 * pre * (1.0 - th * th) * (
            0.7978845608028654 + 0.10703222440890037 * sq
        )
        act_s[rows, :] = act
        y_s[rows, :] += dot(act, wproj)
        du = (dot(cot_ref[rows, :], wproj, 1, 1) * slope).astype(BF16)
        du_s[rows, :] = du
        g_s[rows, :] += dot(du, wfc, 1, 1)
        return sums + jnp.sum(du.astype(F32), axis=0, keepdims=True)

    dfcb_ref[0] = lax.fori_loop(0, tiles, body, jnp.zeros((1, CHUNK), F32))
    dwproj_ref[...] = dot(act_s[...], cot_ref[...], 0, 0).astype(BF16)
    dwfc = dot(h_s[...], du_s[...], 0, 0).astype(BF16)
    share = dwfc_ref.shape[2]
    for f in range(dwfc_ref.shape[0]):
        dwfc_ref[f, 0] = dwfc[f * share : (f + 1) * share, :]

    @pl.when(chunk == pl.num_programs(0) - 1)
    def _():
        def finish(t, sums):
            rows = rows_of(t)
            out_ref[rows, :] = y_s[rows, :].astype(BF16)
            cot = cot_ref[rows, :].astype(F32)
            grad = g_s[rows, :]
            _, normed, inv_std = layer_norm(r_s[rows, :], gain, bias)
            gnorm = grad * gain
            resid = cot + inv_std * (
                gnorm
                - jnp.mean(gnorm, axis=-1, keepdims=True)
                - normed * jnp.mean(gnorm * normed, axis=-1, keepdims=True)
            )
            dr_ref[rows, :] = resid
            branch = resid.astype(BF16)
            do_s[rows, :] = branch
            dc_ref[rows, :] = dot(branch, wout_ref[...], 1, 1).astype(BF16)
            return (
                sums[0] + jnp.sum(grad * normed, axis=0, keepdims=True),
                sums[1] + jnp.sum(grad, axis=0, keepdims=True),
                sums[2] + jnp.sum(cot, axis=0, keepdims=True),
            )

        zero = jnp.zeros((1, x_ref.shape[1]), F32)
        sums = lax.fori_loop(0, tiles, finish, (zero, zero, zero))
        index = lax.broadcasted_iota(jnp.int32, (8, 1), 0)
        vecg_ref[...] = jnp.where(
            index == 0,
            sums[0],
            jnp.where(index == 1, sums[1], jnp.where(index == 2, sums[2], 0.0)),
        )
        dwout_ref[...] = dot(c_ref[...], do_s[...], 0, 0).astype(BF16)


def middle(x, cot, ctx, w_out, w_fc, w_proj, vecs, fc_bias, group):
    rows, dim = x.shape
    hidden = w_fc.shape[1]
    steps = hidden // CHUNK
    share = dim // group

    def fixed(shape):
        return pl.BlockSpec(shape, lambda c: (0,) * len(shape), pipeline_mode=pl.Buffered(1))

    return pl.pallas_call(
        middle_kernel,
        grid=(steps,),
        in_specs=[
            fixed((rows, dim)),
            fixed((rows, dim)),
            fixed((rows, dim)),
            fixed((dim, dim)),
            pl.BlockSpec((dim, CHUNK), lambda c: (0, c)),
            pl.BlockSpec((CHUNK, dim), lambda c: (c, 0)),
            fixed((8, dim)),
            pl.BlockSpec((1, 1, CHUNK), lambda c: (c, 0, 0)),
        ],
        out_specs=[
            fixed((rows, dim)),
            fixed((rows, dim)),
            fixed((rows, dim)),
            fixed((dim, dim)),
            pl.BlockSpec((group, 1, share, CHUNK), lambda c: (0, c, 0, 0)),
            pl.BlockSpec((CHUNK, dim), lambda c: (c, 0)),
            pl.BlockSpec((1, 1, CHUNK), lambda c: (c, 0, 0)),
            fixed((8, dim)),
        ],
        out_shape=[
            jax.ShapeDtypeStruct((rows, dim), BF16),
            jax.ShapeDtypeStruct((rows, dim), F32),
            jax.ShapeDtypeStruct((rows, dim), BF16),
            jax.ShapeDtypeStruct((dim, dim), BF16),
            jax.ShapeDtypeStruct((group, steps, share, CHUNK), BF16),
            jax.ShapeDtypeStruct((hidden, dim), BF16),
            jax.ShapeDtypeStruct((steps, 1, CHUNK), F32),
            jax.ShapeDtypeStruct((8, dim), F32),
        ],
        scratch_shapes=[
            pltpu.VMEM((rows, dim), F32),
            pltpu.VMEM((rows, dim), BF16),
            pltpu.VMEM((rows, dim), F32),
            pltpu.VMEM((rows, dim), F32),
            pltpu.VMEM((rows, CHUNK), BF16),
            pltpu.VMEM((rows, CHUNK), BF16),
            pltpu.VMEM((rows, dim), BF16),
        ],
        compiler_params=params(),
        cost_estimate=pl.CostEstimate(
            flops=12 * rows * dim * hidden, bytes_accessed=40_000_000, transcendentals=0
        ),
        name="middle",
    )(x, cot, ctx, w_out, w_fc, w_proj, vecs, fc_bias)


def attend(q, kv, dcol, drow, stats, ext):
    micro, tok, dim = q.shape
    total = kv.shape[1]
    pairs = dim // 128
    blocks = tok // BLK
    return pl.pallas_call(
        partial(forward_kernel, ext=ext),
        grid=(micro, pairs),
        in_specs=[
            pl.BlockSpec((1, tok, 128), lambda m, p: (m, 0, p)),
            pl.BlockSpec((1, total, 128), lambda m, p: (m, 0, p)),
            pl.BlockSpec((1, total, 128), lambda m, p: (m, 0, pairs + p)),
            pl.BlockSpec((1, ext, 1), lambda m, p: (m, 0, 0)),
            pl.BlockSpec((1, 1, ext), lambda m, p: (m, 0, 0)),
            pl.BlockSpec((1, tok, 128), lambda m, p: (m, 0, 0)),
        ],
        out_specs=[
            pl.BlockSpec((1, tok, 128), lambda m, p: (m, 0, p)),
            pl.BlockSpec((1, 2, blocks, BLK, 2 * BLK), lambda m, p: (m, p, 0, 0, 0)),
            pl.BlockSpec((1, 2, tok, total - ext), lambda m, p: (m, p, 0, 0)),
        ],
        out_shape=[
            jax.ShapeDtypeStruct((micro, tok, dim), BF16),
            jax.ShapeDtypeStruct((micro, 2 * pairs, blocks, BLK, 2 * BLK), BF16),
            jax.ShapeDtypeStruct((micro, 2 * pairs, tok, total - ext), BF16),
        ],
        compiler_params=params(),
        cost_estimate=pl.CostEstimate(
            flops=8 * micro * tok * 768 * dim, bytes_accessed=30_000_000, transcendentals=0
        ),
        name="attend",
    )(q, kv, kv, dcol, drow, stats)


def attend_back(dctx, q, kv, probs, density, stats, km, ks, mean_wide, spread_wide, ext):
    micro, tok, dim = q.shape
    total = kv.shape[1]
    pairs = dim // 128
    blocks = tok // BLK
    basis = total - ext
    part = pl.BlockSpec((1, tok, 128), lambda m, p: (m, 0, p))
    rows = pl.BlockSpec((1, total, 128), lambda m, p: (m, 0, p))
    line = pl.BlockSpec((1, 1, 128), lambda m, p: (m, 0, p))
    wide = pl.BlockSpec((basis, 128), lambda m, p: (0, p))
    return pl.pallas_call(
        partial(backward_kernel, ext=ext),
        grid=(micro, pairs),
        in_specs=[
            part,
            part,
            rows,
            pl.BlockSpec((1, total, 128), lambda m, p: (m, 0, pairs + p)),
            pl.BlockSpec((1, 2, blocks, BLK, 2 * BLK), lambda m, p: (m, p, 0, 0, 0)),
            pl.BlockSpec((1, 2, tok, basis), lambda m, p: (m, p, 0, 0)),
            pl.BlockSpec((1, tok, 128), lambda m, p: (m, 0, 0)),
            line,
            line,
            wide,
            wide,
        ],
        out_specs=[part, rows, rows, pl.BlockSpec((1, 8, 128), lambda m, p: (m, 0, p))],
        out_shape=[
            jax.ShapeDtypeStruct((micro, tok, dim), BF16),
            jax.ShapeDtypeStruct((micro, total, dim), BF16),
            jax.ShapeDtypeStruct((micro, total, dim), BF16),
            jax.ShapeDtypeStruct((micro, 8, dim), F32),
        ],
        scratch_shapes=[pltpu.VMEM((total, 128), F32), pltpu.VMEM((total, 128), F32)],
        compiler_params=params(),
        cost_estimate=pl.CostEstimate(
            flops=16 * micro * tok * 768 * dim, bytes_accessed=30_000_000, transcendentals=0
        ),
        name="attend_back",
    )(dctx, q, kv, kv, probs, density, stats, km, ks, mean_wide, spread_wide)


def on_device(
    tokens,
    cotangent,
    doc_ids,
    positions,
    w_qkv,
    w_out,
    w_fc,
    w_proj,
    ln1_gain,
    ln1_bias,
    ln2_gain,
    ln2_bias,
    fc_bias,
    proj_bias,
    mean_weight,
    spread_weight,
):
    group = lax.axis_size("fsdp")
    member = lax.axis_index("fsdp")
    micro, tok, dim = tokens.shape[0], tokens.shape[2], tokens.shape[3]
    hidden = w_fc.shape[1]
    heads = mean_weight.shape[1]
    basis = mean_weight.shape[0] * group
    head_dim = dim // heads
    seq_len = tok * group
    own_count = positions.shape[2] // group
    first_row = member * tok
    ext = tok + BLK
    x = tokens[:, 0]
    cot = cotangent[:, 0]

    onward = [(i, i + 1) for i in range(group - 1)]
    edge = lax.ppermute(x[:, tok - BLK :], "fsdp", onward)
    sample_pos = positions[:, 0]
    own_rows = lax.dynamic_slice_in_dim(sample_pos, member * own_count, own_count, 1) - first_row
    hot = (own_rows[:, :, None] == jnp.arange(tok)[None, None, :]).astype(BF16)
    picked = jnp.einsum("mst,mtd->msd", hot, x, preferred_element_type=F32).astype(BF16)
    picked = lax.all_gather(picked, "fsdp", axis=1, tiled=True)

    small = [ln1_gain, ln1_bias, ln2_gain, ln2_bias, fc_bias, proj_bias]
    small = small + [mean_weight.reshape(-1), spread_weight.reshape(-1)]
    packed = lax.all_gather(jnp.concatenate(small), "fsdp", axis=0, tiled=False)
    vectors, at = [], 0
    for piece in small:
        vectors.append(packed[:, at : at + piece.shape[0]].reshape(-1).astype(F32))
        at = at + piece.shape[0]
    gain_one, bias_one, gain_two, bias_two, hidden_bias, output_bias = vectors[:6]
    mean_f32 = vectors[6].reshape(basis, heads)
    spread_f32 = vectors[7].reshape(basis, heads)
    full_qkv, full_out, full_fc, full_proj = (
        lax.all_gather(w, "fsdp", axis=0, tiled=True) for w in (w_qkv, w_out, w_fc, w_proj)
    )

    table = basis_rows(sample_pos, seq_len, basis)
    if sample_pos.shape[1] < basis:
        system = jnp.einsum("msn,mtn->mst", table, table, precision=HIGHEST)
        system = system + RIDGE_TERM * jnp.eye(sample_pos.shape[1], dtype=F32)
        solver = jnp.einsum("msn,mst->mnt", table, spd_inverse(system), precision=HIGHEST)
    else:
        system = jnp.einsum("msn,msk->mnk", table, table, precision=HIGHEST)
        system = system + RIDGE_TERM * jnp.eye(basis, dtype=F32)
        solver = jnp.einsum("mkn,msn->mks", spd_inverse(system), table, precision=HIGHEST)

    inputs = x.astype(F32)
    own_low = layer_norm(inputs, gain_one, bias_one)[0].astype(BF16)
    edge_low = layer_norm(edge.astype(F32), gain_one, bias_one)[0].astype(BF16)
    picked_low = layer_norm(picked.astype(F32), gain_one, bias_one)[0].astype(BF16)
    coeff = jnp.einsum("mns,msd->mnd", solver, picked_low.astype(F32), precision=HIGHEST)
    rows_low = jnp.concatenate([edge_low, own_low, coeff.astype(BF16)], axis=1)
    q = jnp.einsum(
        "mtd,de->mte", own_low, full_qkv[:, :dim], preferred_element_type=F32
    ).astype(BF16)
    kv = jnp.einsum(
        "mtd,de->mte", rows_low, full_qkv[:, dim:], preferred_element_type=F32
    ).astype(BF16)

    mean_wide = jnp.repeat(mean_f32, head_dim, axis=1)
    spread_wide = jnp.repeat(spread_f32, head_dim, axis=1)
    mem_keys = kv[:, ext:, :dim].astype(F32)
    km = jnp.sum(mem_keys * mean_wide, axis=1) * head_dim ** (-0.5)
    ks = jnp.sum(mem_keys * spread_wide, axis=1) * head_dim ** (-0.5)
    owner = (jnp.arange(dim)[:, None] // head_dim == jnp.arange(heads)[None, :]).astype(F32)
    both = jnp.concatenate([km[:, :, None] * owner, ks[:, :, None] * owner], axis=2)
    logits = jnp.einsum("mtd,mdj->mtj", q.astype(F32), both, precision=HIGHEST)
    middle_at = jax.nn.sigmoid(logits[:, :, :heads])
    basis_var = (1.25 / basis) ** 2
    spread_logit = logits[:, :, heads:]
    spread_sq = basis_var + SIGMA_SCALE * jax.nn.softplus(spread_logit)
    inv_two = 0.5 / spread_sq
    spread_slope = SIGMA_SCALE * jax.nn.sigmoid(spread_logit)
    columns = [
        middle_at,
        inv_two,
        jnp.sqrt(basis_var / spread_sq),
        -2.0 * inv_two * middle_at * (1.0 - middle_at),
        2.0 * inv_two * inv_two * spread_slope,
        -inv_two * spread_slope,
    ]
    stats = jnp.concatenate(
        [jnp.pad(c, ((0, 0), (0, 0), (0, 16 - heads))) for c in columns]
        + [jnp.zeros((micro, tok, 32), F32)],
        axis=2,
    )

    padded = jnp.concatenate([jnp.full((micro, BLK), -1, jnp.int32), doc_ids[:, 0]], axis=1)
    ext_docs = lax.dynamic_slice_in_dim(padded, first_row, ext, 1)
    ctx, probs, density = attend(
        q, kv, ext_docs[:, :, None], ext_docs[:, None, :], stats, ext
    )

    vecs = jnp.concatenate(
        [v[None] for v in (gain_two, bias_two, output_bias)] + [jnp.zeros((5, dim), F32)]
    )
    rows = micro * tok
    output, d_resid, d_ctx, dw_out, dw_fc, dw_proj, d_hidden, d_vecs = middle(
        x.reshape(rows, dim),
        cot.reshape(rows, dim),
        ctx.reshape(rows, dim),
        full_out,
        full_fc,
        full_proj,
        vecs,
        hidden_bias.reshape(-1, 1, CHUNK),
        group,
    )

    both_axes = ("fsdp", "rep")

    def reduced(parts):
        own = lax.psum_scatter(parts, both_axes, scatter_dimension=0, tiled=True)
        return lax.all_gather(own, "rep", axis=0, tiled=True)

    sum_proj = reduced(dw_proj)
    sum_fc = reduced(dw_fc.reshape(-1, CHUNK))

    d_q, d_k, d_v, d_sums = attend_back(
        d_ctx.reshape(micro, tok, dim),
        q,
        kv,
        probs,
        density,
        stats,
        km[:, None],
        ks[:, None],
        mean_wide,
        spread_wide,
        ext,
    )
    mean_term = jnp.sum(mem_keys * d_sums[:, 0:1], axis=0) * head_dim ** (-0.5)
    spread_term = jnp.sum(mem_keys * d_sums[:, 1:2], axis=0) * head_dim ** (-0.5)
    acc_mean = jnp.dot(mean_term, owner, precision=HIGHEST)
    acc_spread = jnp.dot(spread_term, owner, precision=HIGHEST)

    def back(grad, low, high):
        return jnp.einsum(
            "mte,de->mtd", grad, full_qkv[:, low:high], preferred_element_type=F32
        )

    d_rows = back(d_k, dim, 2 * dim) + back(d_v, 2 * dim, 3 * dim)
    returned = lax.ppermute(
        d_rows[:, :BLK].astype(BF16), "fsdp", [(i + 1, i) for i in range(group - 1)]
    )
    d_picked = jnp.einsum("mns,mnd->msd", solver, d_rows[:, ext:], precision=HIGHEST)
    d_picked = lax.psum_scatter(
        d_picked.astype(BF16), "fsdp", scatter_dimension=1, tiled=True
    )

    def flat(value):
        return value.reshape(-1, value.shape[-1])

    dw_q = dot(flat(own_low), flat(d_q), 0, 0).astype(BF16)
    dw_k = dot(flat(rows_low), flat(d_k), 0, 0).astype(BF16)
    dw_v = dot(flat(rows_low), flat(d_v), 0, 0).astype(BF16)
    last = jnp.stack([v.reshape(group, -1, dim) for v in (dw_out, dw_q, dw_k, dw_v)], axis=1)
    sum_last = reduced(last.reshape(-1, dim)).reshape(4, -1, dim)

    d_first = d_rows[:, BLK:ext] + back(d_q, 0, dim)
    d_first = d_first + jnp.einsum("mst,msd->mtd", hot, d_picked, preferred_element_type=F32)
    d_first = d_first + jnp.pad(returned.astype(F32), ((0, 0), (tok - BLK, 0), (0, 0)))
    _, normed, inv_std = layer_norm(inputs, gain_one, bias_one)
    g_norm = d_first * gain_one
    grad_tokens = d_resid.reshape(micro, tok, dim) + inv_std * (
        g_norm
        - jnp.mean(g_norm, axis=-1, keepdims=True)
        - normed * jnp.mean(g_norm * normed, axis=-1, keepdims=True)
    )
    acc_gain_one = jnp.sum(d_first * normed, axis=(0, 1))
    acc_bias_one = jnp.sum(d_first, axis=(0, 1))

    vector_parts = [
        acc_gain_one,
        acc_bias_one,
        d_vecs[0],
        d_vecs[1],
        d_hidden,
        d_vecs[2],
        acc_mean,
        acc_spread,
    ]
    joined = jnp.concatenate([v.reshape(group, -1) for v in vector_parts], axis=1)
    joined = lax.psum(joined, both_axes)
    own = lax.dynamic_slice_in_dim(joined, member, 1, 0)[0]
    pieces, at = [], 0
    for part in vector_parts:
        size = part.size // group
        pieces.append(own[at : at + size])
        at = at + size
    share = dim // group
    grad_fc = sum_fc.reshape(hidden // CHUNK, share, CHUNK).transpose(1, 0, 2)
    grad_qkv = jnp.concatenate([sum_last[1], sum_last[2], sum_last[3]], axis=1)
    return (
        output.reshape(micro, 1, tok, dim),
        grad_tokens[:, None],
        grad_qkv.astype(F32),
        sum_last[0].astype(F32),
        grad_fc.reshape(share, hidden).astype(F32),
        sum_proj.astype(F32),
        pieces[0],
        pieces[1],
        pieces[2],
        pieces[3],
        pieces[4],
        pieces[5],
        pieces[6].reshape(-1, heads),
        pieces[7].reshape(-1, heads),
    )


def solution(mesh):
    seq = P(None, "rep", "fsdp", None)
    row = P("fsdp", None)
    vec = P("fsdp")
    return jax.shard_map(
        on_device,
        mesh=mesh,
        in_specs=(seq, seq, P(None, "rep", None), P(None, "rep", None))
        + (row, row, row, row)
        + (vec,) * 6
        + (row, row),
        out_specs=(seq, seq, row, row, row, row) + (vec,) * 6 + (row, row),
        check_vma=False,
    )
```

time: 1190 us -> 782 us (0.66)
  matrix products: 371 us -> 45.6 us
  other arithmetic: 203 us -> 29.2 us
  Pallas kernels: 0 us -> 151 us
  waiting for transfers between devices: 263 us -> 402 us
  blocking collectives: 180 us -> 82.8 us
  local copies, waits for them, and re-layouts: 134 us -> 45.7 us
    dot_general x68 -> x17, matrix products: 346 us -> 45.6 us  [the longest x3 14.9 us: back(): jnp.einsum('mte,de->mtd', grad, full_qkv[:, low:high], preferred_element_...]
    reduce_scatter x4, waiting for transfers between devices: 0.03 us -> 273 us  [the longest x3 259 us: reduced(): own = lax.psum_scatter(parts, both_axes, scatter_dimension=0, tiled=True)]
    unnamed x15 -> x11, waiting for transfers between devices: 224 us -> 2.87 us
    pallas_call x0 -> x4, Pallas kernels: none -> 151 us  [the longest x1 58.3 us: middle(): pl.pallas_call(middle_kernel, grid=(steps,), in_specs=[fixed((rows, dim))...]
    all_gather x7, waiting for transfers between devices: 0.05 us -> 126 us  [the longest x4 71.3 us: on_device(): lax.all_gather(w, 'fsdp', axis=0, tiled=True)]
    unnamed x3 -> x0, blocking collectives: 124 us -> none
    another operation x28 -> x1, other arithmetic: 114 us -> 0.64 us  [on_device(): jnp.stack([v.reshape(group, -1, dim) for v in (dw_out, dw_q, dw_k, dw_v)]...]
    psum x0 -> x1, blocking collectives: none -> 40.4 us  [on_device(): joined = lax.psum(joined, both_axes)]
  transfers between devices with their start and end apart: 18 -> 13, of which waited for: 4 -> 8; matrix products, arithmetic and copies ran while one was open for 40% -> 15% of each run, Pallas kernels for 0% -> 12%
where the time goes in v1:
time: 782 us; the launch traced here: 778 us
  waiting for transfers between devices  402 us (51%)
  Pallas kernels  151 us (19%)
  blocking collectives  82.8 us (11%)
  local copies, waits for them, and re-layouts  45.7 us (6%)
  matrix products  45.6 us (6%)
  other arithmetic  29.2 us (4%)
  between operations  14.9 us (2%)
    reduce_scatter x3, waiting for transfers between devices, reduced(): own = lax.psum_scatter(parts, both_axes, scatter_dimension=0, tiled=True)  259 us
    all_gather x4, waiting for transfers between devices, on_device(): lax.all_gather(w, 'fsdp', axis=0, tiled=True)  71.3 us
    pallas_call x1, Pallas kernels, middle(): pl.pallas_call(middle_kernel, grid=(steps,), in_specs=[fixed((rows, dim))...  58.3 us
    all_gather x3, waiting for transfers between devices, reduced(): return lax.all_gather(own, 'rep', axis=0, tiled=True)  54.3 us
    psum x1, blocking collectives, on_device(): joined = lax.psum(joined, both_axes)  40.4 us
    pallas_call x1, Pallas kernels, attend_back(): pl.pallas_call(partial(backward_kernel, ext=ext), grid=(micro, pairs), in...  38.4 us
    all_gather x1, blocking collectives, on_device(): picked = lax.all_gather(picked, 'fsdp', axis=1, tiled=True)  36.7 us
    pallas_call x1, Pallas kernels, attend(): pl.pallas_call(partial(forward_kernel, ext=ext), grid=(micro, pairs), in_...  28.1 us
  transfers between devices with their start and end apart: 13, of which 8 were waited for; matrix products, arithmetic and copies ran while one was open for 15% of the time, Pallas kernels for 12%

profile of v1, /device:TPU:0, one launch (start us, length us, event | category | flops | bytes accessed | tf_op | source)
XLA Modules:
  0.0 778.1 jit_solution(13632648763880603386)
XLA Ops:
  7.2 0.7 all-gather.10.cloned.1.call-update
  8.0 0.7 all-gather.12.cloned.1.call-update
  8.7 0.7 all-gather.14.cloned.1.call-update
  9.5 0.9 slice.179
  10.5 5.1 collective-permute-start
  16.5 36.7 %all_gather.33 = bf16[2,128,768]{2,1,0:T(8,128)(2,1)S(1)} all-gather(bf16[2,64,768]{2,1,0:T(8,128)(2,1)S(1)} %convolution_convert_fusion.3), channel_id=1, replica_groups=mesh['rep'=16,'fsdp'=2] {'fsdp'}, dimensions={1}, use_global_device_ids=true | all-gather | bytes 589824 | tf_op jit(solution)/shard_map/all_gather | solution.py:442
  56.1 5.7 all-gather.1
  61.8 1.4 convolution_add_fusion.1.a_ref
  63.3 26.5 %inverse.1 = f32[2,128,128]{2,1,0:T(8,128)} custom-call(f32[2,128,128]{2,1,0:T(8,128)} %convolution_add_fusion.1.a_ref), custom_call_target="tpu_custom_call" | custom-call | flops 20000000 | bytes 300000 | tf_op jit(solution)/shard_map/inverse/pallas_call | solution.py:73
  89.7 1.4 fusion.58
  93.7 1.8 convolution_convert_fusion.2
  97.6 1.0 broadcast_in_dim.16
  98.5 1.4 copy.149.mw_ref
  99.9 0.9 reshape.363
  100.8 0.7 copy.150
  101.5 1.7 broadcast_in_dim.17
  103.2 2.3 copy.151.sw_ref
  105.5 1.9 copy.159.dcol_ref
  108.6 1.8 fusion.7
  110.9 1.2 fusion.22
  112.2 7.9 %convolution_convert_fusion.k_ref.v_ref = bf16[2,1024,1536]{2,1,0:T(8,128)(2,1)S(1)} fusion(bf16[768,2304]{1,0:T(8,128)(2,1)} %all-gather.10.cloned.1.call-done, bf16[2,256,768]{2,1,0:T(8,128)(2,1)} %convolution_convert_fusion.2, bf16[2,512,768]{2,1,0:T(8,128)(2,1)} %fusion.7, bf16[2,256,768]{2,1,0:T(8,128)(2,1)} %fusion.22), kind=kOutput, calls=%fused_computation | convolution fusion | flops 4844421120 | bytes 11796480 | tf_op jit(solution)/shard_map/mtd,de->mte/dot_general | solution.py:477
  120.5 3.6 convolution_convert_fusion.1.q_ref
  124.1 1.4 fusion.59
  125.4 0.9 negate_multiply_fusion
  126.4 0.8 pad.30
  127.3 0.8 pad.31
  128.2 2.8 concatenate.28.st_ref
  131.0 28.1 %attend.1 = (bf16[2,512,768]{2,1,0:T(8,128)(2,1)}, bf16[2,12,2,256,512]{4,3,2,1,0:T(8,128)(2,1)}, bf16[2,12,512,256]{3,2,1,0:T(8,128)(2,1)}) custom-call(bf16[2,512,768]{2,1,0:T(8,128)(2,1)} %copy-done.5, bf16[2,1024,1536]{2,1,0:T(8,128)(2,1)} %copy-done.2, bf16[2,1024,1536]{2,1,0:T(8,128)(2,1)} %copy-done.2, s32[2,768,1]{2,1,0:T(8,128)} %copy.159.dcol_ref, ...), custom_call_target="tpu_custom_call" | custom-call | flops 4831838208 | bytes 30000000 | tf_op jit(solution)/shard_map/attend/pallas_call | solution.py:333
  159.1 7.2 all-gather.14.cloned.1.call-done.wfc_ref
  166.3 64.1 %all-gather.16.cloned.1.call-done.wproj_ref = bf16[3072,768]{1,0:T(8,128)(2,1)} async-done(((bf16[1536,768]{1,0:T(8,128)(2,1)}), bf16[3072,768]{1,0:T(8,128)(2,1)}) %all-gather.16.cloned.1.call-update) | async-done | bytes 4718608 | tf_op jit(solution)/shard_map/all_gather | solution.py:455
  230.3 58.3 %middle.1 = (bf16[1024,768]{1,0:T(8,128)(2,1)}, f32[1024,768]{1,0:T(8,128)}, bf16[1024,768]{1,0:T(8,128)(2,1)}, bf16[768,768]{1,0:T(8,128)(2,1)}, bf16[2,6,384,5...) custom-call(bf16[1024,768]{1,0:T(8,128)(2,1)} %bitcast.98, ...), custom_call_target="tpu_custom_call" | custom-call | flops 28991029248 | bytes 40000000 | tf_op jit(solution)/shard_map/middle/pallas_call | solution.py:278
  289.9 38.4 %attend_back.1 = (bf16[2,512,768]{2,1,0:T(8,128)(2,1)}, bf16[2,1024,768]{2,1,0:T(8,128)(2,1)}, bf16[2,1024,768]{2,1,0:T(8,128)(2,1)}, f32[2,8,768]{2,1,0:T(8,128)}) custom-call(bf16[2,512,768]{2,1,0:T(8,128)(2,1)} %bitcast.107, bf16[2,512,768]{2,1,0:T(8,128)(2,1)} %copy-done.5, bf16[2,1024,1536]{2,1,0:T(8,128)(2,1)} %copy-done.2, ...), custom_call_target="tpu_custom_call" | custom-call | flops 9663676416 | bytes 30000000 | tf_op jit(solution)/shard_map/attend_back/pallas_call | solution.py:372
  328.3 3.0 bitcast_convert_fusion.2
  331.4 2.7 bitcast_convert_fusion.1
  334.1 2.7 bitcast_convert_fusion
  337.4 2.6 copy.167
  340.1 0.7 reduce-scatter.11.cloned.1.call-update
  341.0 5.1 fusion.32
  346.1 4.1 convolution_add_fusion
  350.2 2.7 copy-done.9
  352.8 1.8 fusion.29
  354.7 41.7 %reduce-scatter.9.cloned.1.call-done = bf16[144,512]{1,0:T(8,128)(2,1)} async-done(((bf16[4608,512]{1,0:T(8,128)(2,1)}), bf16[144,512]{1,0:T(8,128)(2,1)}) %reduce-scatter.9.cloned.1.call-update) | async-done | bytes 147472 | tf_op jit(solution)/shard_map/reduce_scatter | solution.py:534
  396.4 111.8 %reduce-scatter.7.cloned.1.call-done = bf16[96,768]{1,0:T(8,128)(2,1)} async-done(((bf16[3072,768]{1,0:T(8,128)(2,1)}), bf16[96,768]{1,0:T(8,128)(2,1)}) %reduce-scatter.7.cloned.1.call-update) | async-done | bytes 147472 | tf_op jit(solution)/shard_map/reduce_scatter | solution.py:534
  508.2 1.5 slice.261
  509.7 1.3 collective-permute-start.1
  511.0 0.9 fusion.85
  511.9 1.7 fusion.26
  514.2 0.9 slice_reduce_fusion
  515.2 105.5 %reduce-scatter.11.cloned.1.call-done = bf16[96,768]{1,0:T(8,128)(2,1)} async-done(((bf16[3072,768]{1,0:T(8,128)(2,1)}), bf16[96,768]{1,0:T(8,128)(2,1)}) %reduce-scatter.11.cloned.1.call-update) | async-done | bytes 147472 | tf_op jit(solution)/shard_map/reduce_scatter | solution.py:534
  621.4 14.3 %reduce-scatter.5.cloned.1.call-done = bf16[2,64,768]{2,1,0:T(8,128)(2,1)} async-done(((bf16[2,128,768]{2,1,0:T(8,128)(2,1)}), bf16[2,64,768]{2,1,0:T(8,128)(2,1)}) %reduce-scatter.5.cloned.1.call-update) | async-done | bytes 196624 | tf_op jit(solution)/shard_map/reduce_scatter | solution.py:568
  635.7 1.8 fusion.57
  637.5 5.8 fusion.13
  643.4 40.4 %psum.7 = f32[2,6528]{1,0:T(2,128)S(1)} all-reduce(f32[2,6528]{1,0:T(2,128)S(1)} %constant_dynamic-update-slice_fusion), channel_id=1, replica_groups=mesh['rep'=16,'fsdp'=2] {'fsdp','rep'}, use_global_device_ids=true, to_apply=%region_18.19 | all-reduce | flops 13056 | bytes 104448 | tf_op jit(solution)/shard_map/psum | solution.py:605
  683.8 0.7 dynamic-slice_reduce_fusion
  686.1 0.7 dynamic-slice_reduce_fusion.3
  686.8 4.6 fusion.12
  691.4 4.5 convert_bitcast_fusion
  695.9 6.0 copy.168
  701.9 6.0 copy.173
  708.0 15.8 %all-gather.18.cloned.1.call-done = bf16[1536,768]{1,0:T(8,128)(2,1)} async-done(((bf16[96,768]{1,0:T(8,128)(2,1)}), bf16[1536,768]{1,0:T(8,128)(2,1)}) %all-gather.18.cloned.1.call-update) | async-done | bytes 2359312 | tf_op jit(solution)/shard_map/all_gather | solution.py:535
  723.8 2.8 slice_convert_fusion.1
  726.6 2.0 maximum_convert_fusion
  728.6 38.5 %all-gather.22.cloned.1.call-done = bf16[1536,768]{1,0:T(8,128)(2,1)} async-done(((bf16[96,768]{1,0:T(8,128)(2,1)}), bf16[1536,768]{1,0:T(8,128)(2,1)}) %all-gather.22.cloned.1.call-update) | async-done | bytes 2359312 | tf_op jit(solution)/shard_map/all_gather | solution.py:535
  767.1 4.2 convert_element_type.223
  (176 shorter events, 16.3 us)
Async XLA Ops:
  7.2 2.3 copy-start
  7.2 105.0 %all-gather.10.cloned.1.call-start = ((), (), s32[]{:S(2)}) async-start(), calls=%async_computation.4 | async-start | bytes 5308416 | tf_op jit(solution)/shard_map/all_gather | solution.py:455
  7.9 151.2 %all-gather.12.cloned.1.call-start = ((), (), s32[]{:S(2)}) async-start(), calls=%async_computation.5 | async-start | bytes 1769472 | tf_op jit(solution)/shard_map/all_gather | solution.py:455
  8.7 157.6 %all-gather.14.cloned.1.call-start = ((), (), s32[]{:S(2)}) async-start(), calls=%async_computation.6 | async-start | bytes 7077888 | tf_op jit(solution)/shard_map/all_gather | solution.py:455
  9.4 6.5 copy-start.23
  9.4 220.9 %all-gather.16.cloned.1.call-start = ((), (), s32[]{:S(2)}) async-start(), calls=%async_computation.7 | async-start | bytes 7077888 | tf_op jit(solution)/shard_map/all_gather | solution.py:455
  10.4 43.2 %copy-start.20 = (bf16[128,12]{0,1:T(8,128)(2,1)S(1)}, bf16[128,12]{0,1:T(8,128)(2,1)}, u32[]{:S(2)}) copy-start(bf16[128,12]{0,1:T(8,128)(2,1)} %param.30) | copy-start | bytes 9220
  10.4 43.4 %copy-start.21 = (bf16[128,12]{0,1:T(8,128)(2,1)S(1)}, bf16[128,12]{0,1:T(8,128)(2,1)}, u32[]{:S(2)}) copy-start(bf16[128,12]{0,1:T(8,128)(2,1)} %param.31) | copy-start | bytes 9220
  10.4 43.7 %copy-start.24 = (bf16[384]{0:T(512)(128)(2,1)S(1)}, bf16[384]{0:T(512)(128)(2,1)}, u32[]{:S(2)}) copy-start(bf16[384]{0:T(512)(128)(2,1)} %param.24) | copy-start | bytes 2308
  10.4 43.9 %copy-start.25 = (bf16[384]{0:T(512)(128)(2,1)S(1)}, bf16[384]{0:T(512)(128)(2,1)}, u32[]{:S(2)}) copy-start(bf16[384]{0:T(512)(128)(2,1)} %param.25) | copy-start | bytes 2308
  10.4 44.2 %copy-start.26 = (bf16[384]{0:T(512)(128)(2,1)S(1)}, bf16[384]{0:T(512)(128)(2,1)}, u32[]{:S(2)}) copy-start(bf16[384]{0:T(512)(128)(2,1)} %param.26) | copy-start | bytes 2308
  10.4 44.4 %copy-start.27 = (bf16[384]{0:T(512)(128)(2,1)S(1)}, bf16[384]{0:T(512)(128)(2,1)}, u32[]{:S(2)}) copy-start(bf16[384]{0:T(512)(128)(2,1)} %param.27) | copy-start | bytes 2308
  10.4 44.6 %copy-start.22 = (bf16[1536]{0:T(1024)(128)(2,1)S(1)}, bf16[1536]{0:T(1024)(128)(2,1)}, u32[]{:S(2)}) copy-start(bf16[1536]{0:T(1024)(128)(2,1)} %param.28) | copy-start | bytes 9220
  10.5 44.8 %copy-start.28 = (bf16[384]{0:T(512)(128)(2,1)S(1)}, bf16[384]{0:T(512)(128)(2,1)}, u32[]{:S(2)}) copy-start(bf16[384]{0:T(512)(128)(2,1)} %param.29) | copy-start | bytes 2308
  10.5 99.9 %collective-permute-start = (bf16[2,256,768]{2,1,0:T(8,128)(2,1)}, bf16[2,256,768]{2,1,0:T(8,128)(2,1)S(1)}, u32[]{:S(2)}, u32[]{:S(2)}) collective-permute-start(bf16[2,256,768]{2,1,0:T(8,128)(2,1)} %slice.179), channel_id=1, source_target_pairs={{0,1},{2,3},{4,5},{6,7},{8,9},{10,11},{12,13},{14,15},{16,17},{18,... | collective-permute-start | bytes 2359304 | tf_op jit(solution)/shard_map/ppermute | solution.py:437
  15.5 380.8 %reduce-scatter.9.cloned.1.call-start = ((), (), s32[]{:S(2)}) async-start(), calls=%async_computation.11 | async-start | bytes 4866048 | tf_op jit(solution)/shard_map/reduce_scatter | solution.py:534
  16.0 37.5 %copy-start.17 = (s32[2,1,64]{2,1,0:T(1,128)}, s32[2,1,64]{2,1,0:T(1,128)S(1)}, u32[]{:S(2)}) copy-start(s32[2,1,64]{2,1,0:T(1,128)S(1)} %dynamic-slice_subtract_fusion) | copy-start | bytes 1540
  16.0 76.9 %copy-start.19 = (s32[2,1,1024]{2,1,0:T(1,128)S(1)}, s32[2,1,1024]{2,1,0:T(1,128)}, u32[]{:S(2)}) copy-start(s32[2,1,1024]{2,1,0:T(1,128)} %param.18) | copy-start | bytes 24580
  99.9 20.1 %copy-start.3 = (f32[256,768]{1,0:T(8,128)}, f32[256,768]{1,0:T(8,128)S(1)}, u32[]{:S(2)}) copy-start(f32[256,768]{1,0:T(8,128)S(1)} %copy.149.mw_ref) | copy-start | bytes 2359300
  101.5 5.8 copy-start.15
  101.5 6.4 copy-start.13
  101.5 7.1 copy-start.14
  112.2 7.9 %copy-start.4 = (f32[256,768]{1,0:T(8,128)S(1)}, f32[256,768]{1,0:T(8,128)}, u32[]{:S(2)}) copy-start(f32[256,768]{1,0:T(8,128)} %copy.151.sw_ref) | copy-start | bytes 2359300
  112.2 8.2 %copy-start.12 = (f32[768,12]{0,1:T(8,128)S(1)}, f32[768,12]{0,1:T(8,128)}, u32[]{:S(2)}) copy-start(f32[768,12]{0,1:T(8,128)} %fusion.72) | copy-start | bytes 110596
  112.2 8.3 %copy-start.6 = (bf16[2,512,768]{2,1,0:T(8,128)(2,1)S(1)}, bf16[2,512,768]{2,1,0:T(8,128)(2,1)}, u32[]{:S(2)}) copy-start(bf16[2,512,768]{2,1,0:T(8,128)(2,1)} %fusion.7) | copy-start | bytes 4718596
  120.1 4.0 copy-start.2
  124.0 2.3 copy-start.5
  288.7 219.5 %reduce-scatter.7.cloned.1.call-start = ((), (), s32[]{:S(2)}) async-start(), calls=%async_computation.9 | async-start | bytes 4866048 | tf_op jit(solution)/shard_map/reduce_scatter | solution.py:534
  289.9 38.4 %copy-start.7 = (bf16[2,512,768]{2,1,0:T(8,128)(2,1)S(1)}, bf16[2,512,768]{2,1,0:T(8,128)(2,1)}, u32[]{:S(2)}) copy-start(bf16[2,512,768]{2,1,0:T(8,128)(2,1)} %fusion.7) | copy-start | bytes 4718596
  328.3 3.1 copy-start.10
  328.3 3.1 copy-start.11
  328.3 3.1 copy-start.31
  331.4 2.7 copy-start.29
  334.1 2.7 copy-start.8
  340.0 280.7 %reduce-scatter.11.cloned.1.call-start = ((), (), s32[]{:S(2)}) async-start(), calls=%async_computation.13 | async-start | bytes 4866048 | tf_op jit(solution)/shard_map/reduce_scatter | solution.py:534
  340.8 5.3 copy-start.30
  340.8 294.9 %reduce-scatter.5.cloned.1.call-start = ((), (), s32[]{:S(2)}) async-start(), calls=%async_computation.8 | async-start | bytes 589824 | tf_op jit(solution)/shard_map/reduce_scatter | solution.py:568
  350.2 2.7 copy-start.9
  354.6 160.6 %copy-start.16 = (f32[6,1,512]{2,1,0:T(1,128)S(1)}, f32[6,1,512]{2,1,0:T(1,128)}, u32[]{:S(2)}) copy-start(f32[6,1,512]{2,1,0:T(1,128)} %get-tuple-element.42) | copy-start | bytes 36868
  354.6 336.8 %all-gather.20.cloned.1.call-start = ((), (), s32[]{:S(2)}) async-start(), calls=%async_computation.12 | async-start | bytes 2506752 | tf_op jit(solution)/shard_map/all_gather | solution.py:535
  396.4 327.4 %all-gather.18.cloned.1.call-start = ((), (), s32[]{:S(2)}) async-start(), calls=%async_computation.10 | async-start | bytes 2506752 | tf_op jit(solution)/shard_map/all_gather | solution.py:535
  508.2 258.9 %all-gather.22.cloned.1.call-start = ((), (), s32[]{:S(2)}) async-start(), calls=%async_computation.14 | async-start | bytes 2506752 | tf_op jit(solution)/shard_map/all_gather | solution.py:535
  508.2 127.5 %copy-start.18 = (s32[2,1,64]{2,1,0:T(1,128)S(1)}, s32[2,1,64]{2,1,0:T(1,128)}, u32[]{:S(2)}) copy-start(s32[2,1,64]{2,1,0:T(1,128)} %copy-done.17) | copy-start | bytes 1540
  509.7 127.7 %collective-permute-start.1 = (bf16[2,256,768]{2,1,0:T(8,128)(2,1)S(1)}, bf16[2,256,768]{2,1,0:T(8,128)(2,1)}, u32[]{:S(2)}, u32[]{:S(2)}) collective-permute-start(bf16[2,256,768]{2,1,0:T(8,128)(2,1)S(1)} %slice.261), channel_id=1, source_target_pairs={{1,0},{3,2},{5,4},{7,6},{9,8},{11,10},{13,12},{15,14},{17,16},{19,... | collective-permute-start | bytes 2359304 | tf_op jit(solution)/shard_map/ppermute | solution.py:564
  513.6 123.9 %copy-start.1 = (bf16[2,1,512,768]{3,2,1,0:T(8,128)(2,1)S(1)}, bf16[2,1,512,768]{3,2,1,0:T(8,128)(2,1)}, u32[]{:S(2)}) copy-start(bf16[2,1,512,768]{3,2,1,0:T(8,128)(2,1)} %param.16) | copy-start | bytes 4718596
  635.7 1.8 copy-start.32
Sparse Core Ops, SparseCore 0:
  9.5 65.7 all-gather.9
  76.8 25.1 all-gather.11
  103.6 62.6 all-gather.13
  167.7 62.6 all-gather.15
  288.8 107.5 reduce-scatter.8
  401.7 106.4 reduce-scatter.6
  514.2 106.4 reduce-scatter.10
  623.5 12.1 reduce-scatter.4
  638.0 42.3 all-gather.19
  682.6 41.1 all-gather.17
  726.1 41.0 all-gather.21

commit v2 on v1

--- a/solution.py
+++ b/solution.py
@@ -30,6 +30,71 @@
 
 def params(limit=VMEM_BYTES):
     return pltpu.CompilerParams(vmem_limit_bytes=limit)
+
+
+def bits_of(axis):
+    return range(lax.axis_size(axis).bit_length() - 1)
+
+
+def side(axis, bit):
+    return (lax.axis_index(axis) >> bit) & 1
+
+
+def swapped(value, axis, bit):
+    return lax.ppermute(value, axis, [(i, i ^ (1 << bit)) for i in range(lax.axis_size(axis))])
+
+
+def halved(value, axis, bit, dim):
+    half = value.shape[dim] // 2
+    mine = side(axis, bit)
+    kept = lax.dynamic_slice_in_dim(value, mine * half, half, dim)
+    sent = lax.dynamic_slice_in_dim(value, (1 - mine) * half, half, dim)
+    return kept + swapped(sent, axis, bit)
+
+
+def doubled(value, other, mine, dim):
+    return jnp.where(
+        mine == 0,
+        jnp.concatenate([value, other], axis=dim),
+        jnp.concatenate([other, value], axis=dim),
+    )
+
+
+def gathered(value, axis, dim):
+    for bit in bits_of(axis):
+        value = doubled(value, swapped(value, axis, bit), side(axis, bit), dim)
+    return value
+
+
+def scattered(value, axis, dim):
+    for bit in reversed(bits_of(axis)):
+        value = halved(value, axis, bit, dim)
+    return value
+
+
+def gathered_weight(weight):
+    if lax.axis_size("fsdp") != 2:
+        return lax.all_gather(weight, "fsdp", axis=0, tiled=True)
+    core = side("rep", 0)
+    half = weight.shape[0] // 2
+    sent = lax.dynamic_slice_in_dim(weight, core * half, half, 0)
+    first = swapped(sent, "fsdp", 0)
+    other = doubled(first, swapped(first, "rep", 0), core, 0)
+    return doubled(weight, other, side("fsdp", 0), 0)
+
+
+def reduced(parts, early):
+    own = halved(parts, "rep", 0, 1)
+    order = list(bits_of("rep"))[1:]
+    for bit in order[:early]:
+        own = halved(own, "rep", bit, 1)
+    own = scattered(own, "fsdp", 0)
+    for bit in order[early:]:
+        own = halved(own, "rep", bit, 1)
+    own = own[0]
+    for bit in reversed(bits_of("rep")):
+        own = doubled(own, swapped(own, "rep", bit), side("rep", bit), 0)
+    return own
 
 
 def layer_norm(inputs, gains, offsets):
@@ -74,7 +139,7 @@
         inverse_kernel,
         out_shape=jax.ShapeDtypeStruct(systems.shape, F32),
         compiler_params=params(),
-        cost_estimate=pl.CostEstimate(flops=20_000_000, bytes_accessed=300_000, transcendentals=0),
+        cost_estimate=pl.CostEstimate(flops=26_000_000_000, bytes_accessed=300_000, transcendentals=0),
         name="inverse",
     )(systems)
 
@@ -319,7 +384,7 @@
         ],
         compiler_params=params(),
         cost_estimate=pl.CostEstimate(
-            flops=12 * rows * dim * hidden, bytes_accessed=40_000_000, transcendentals=0
+            flops=24 * rows * dim * hidden, bytes_accessed=40_000_000, transcendentals=0
         ),
         name="middle",
     )(x, cot, ctx, w_out, w_fc, w_proj, vecs, fc_bias)
@@ -353,7 +418,7 @@
         ],
         compiler_params=params(),
         cost_estimate=pl.CostEstimate(
-            flops=8 * micro * tok * 768 * dim, bytes_accessed=30_000_000, transcendentals=0
+            flops=48 * micro * tok * 768 * dim, bytes_accessed=30_000_000, transcendentals=0
         ),
         name="attend",
     )(q, kv, kv, dcol, drow, stats)
@@ -395,7 +460,7 @@
         scratch_shapes=[pltpu.VMEM((total, 128), F32), pltpu.VMEM((total, 128), F32)],
         compiler_params=params(),
         cost_estimate=pl.CostEstimate(
-            flops=16 * micro * tok * 768 * dim, bytes_accessed=30_000_000, transcendentals=0
+            flops=64 * micro * tok * 768 * dim, bytes_accessed=30_000_000, transcendentals=0
         ),
         name="attend_back",
     )(dctx, q, kv, kv, probs, density, stats, km, ks, mean_wide, spread_wide)
@@ -439,11 +504,11 @@
     own_rows = lax.dynamic_slice_in_dim(sample_pos, member * own_count, own_count, 1) - first_row
     hot = (own_rows[:, :, None] == jnp.arange(tok)[None, None, :]).astype(BF16)
     picked = jnp.einsum("mst,mtd->msd", hot, x, preferred_element_type=F32).astype(BF16)
-    picked = lax.all_gather(picked, "fsdp", axis=1, tiled=True)
+    picked = gathered(picked, "fsdp", 1)
 
     small = [ln1_gain, ln1_bias, ln2_gain, ln2_bias, fc_bias, proj_bias]
     small = small + [mean_weight.reshape(-1), spread_weight.reshape(-1)]
-    packed = lax.all_gather(jnp.concatenate(small), "fsdp", axis=0, tiled=False)
+    packed = gathered(jnp.concatenate(small)[None], "fsdp", 0)
     vectors, at = [], 0
     for piece in small:
         vectors.append(packed[:, at : at + piece.shape[0]].reshape(-1).astype(F32))
@@ -452,7 +517,7 @@
     mean_f32 = vectors[6].reshape(basis, heads)
     spread_f32 = vectors[7].reshape(basis, heads)
     full_qkv, full_out, full_fc, full_proj = (
-        lax.all_gather(w, "fsdp", axis=0, tiled=True) for w in (w_qkv, w_out, w_fc, w_proj)
+        gathered_weight(w) for w in (w_qkv, w_out, w_fc, w_proj)
     )
 
     table = basis_rows(sample_pos, seq_len, basis)
@@ -528,14 +593,8 @@
         group,
     )
 
-    both_axes = ("fsdp", "rep")
-
-    def reduced(parts):
-        own = lax.psum_scatter(parts, both_axes, scatter_dimension=0, tiled=True)
-        return lax.all_gather(own, "rep", axis=0, tiled=True)
-
-    sum_proj = reduced(dw_proj)
-    sum_fc = reduced(dw_fc.reshape(-1, CHUNK))
+    sum_proj = reduced(dw_proj.reshape(group, -1, dim), 0)
+    sum_fc = reduced(dw_fc.reshape(group, -1, CHUNK), 1)
 
     d_q, d_k, d_v, d_sums = attend_back(
         d_ctx.reshape(micro, tok, dim),
@@ -565,9 +624,7 @@
         d_rows[:, :BLK].astype(BF16), "fsdp", [(i + 1, i) for i in range(group - 1)]
     )
     d_picked = jnp.einsum("mns,mnd->msd", solver, d_rows[:, ext:], precision=HIGHEST)
-    d_picked = lax.psum_scatter(
-        d_picked.astype(BF16), "fsdp", scatter_dimension=1, tiled=True
-    )
+    d_picked = scattered(d_picked.astype(BF16), "fsdp", 1)
 
     def flat(value):
         return value.reshape(-1, value.shape[-1])
@@ -576,7 +633,7 @@
     dw_k = dot(flat(rows_low), flat(d_k), 0, 0).astype(BF16)
     dw_v = dot(flat(rows_low), flat(d_v), 0, 0).astype(BF16)
     last = jnp.stack([v.reshape(group, -1, dim) for v in (dw_out, dw_q, dw_k, dw_v)], axis=1)
-    sum_last = reduced(last.reshape(-1, dim)).reshape(4, -1, dim)
+    sum_last = reduced(last.reshape(group, -1, dim), 0).reshape(4, -1, dim)
 
     d_first = d_rows[:, BLK:ext] + back(d_q, 0, dim)
     d_first = d_first + jnp.einsum("mst,msd->mtd", hot, d_picked, preferred_element_type=F32)
@@ -602,8 +659,9 @@
         acc_spread,
     ]
     joined = jnp.concatenate([v.reshape(group, -1) for v in vector_parts], axis=1)
-    joined = lax.psum(joined, both_axes)
-    own = lax.dynamic_slice_in_dim(joined, member, 1, 0)[0]
+    own = scattered(joined, "fsdp", 0)[0]
+    for bit in bits_of("rep"):
+        own = own + swapped(own, "rep", bit)
     pieces, at = [], 0
     for part in vector_parts:
         size = part.size // group

time: 782 us -> 531 us (0.68)
  waiting for transfers between devices: 402 us -> 133 us
  blocking collectives: 82.8 us -> 0 us
  starting transfers between devices: 6.95 us -> 49.3 us
  other arithmetic: 29.2 us -> 66.7 us
  local copies, waits for them, and re-layouts: 45.7 us -> 80.1 us
  between operations: 14.9 us -> 2.32 us
    reduce_scatter x4 -> x0, waiting for transfers between devices: 273 us -> none  [the longest x3 259 us: reduced(): own = lax.psum_scatter(parts, both_axes, scatter_dimension=0, tiled=True)]
    ppermute x0 -> x43, waiting for transfers between devices: none -> 133 us  [swapped(): lax.ppermute(value, axis, [(i, i ^ 1 << bit) for i in range(lax.axis_size...]
    all_gather x7 -> x0, waiting for transfers between devices: 126 us -> none  [the longest x4 71.3 us: on_device(): lax.all_gather(w, 'fsdp', axis=0, tiled=True)]
    ppermute x0 -> x43, starting transfers between devices: none -> 46.1 us  [swapped(): lax.ppermute(value, axis, [(i, i ^ 1 << bit) for i in range(lax.axis_size...]
    all_gather x2 -> x0, blocking collectives: 42.4 us -> none  [the longest x1 36.7 us: on_device(): picked = lax.all_gather(picked, 'fsdp', axis=1, tiled=True)]
    psum x1 -> x0, blocking collectives: 40.4 us -> none  [on_device(): joined = lax.psum(joined, both_axes)]
    select_n x0 -> x20, other arithmetic: none -> 28 us  [doubled(): jnp.where(mine == 0, jnp.concatenate([value, other], axis=dim), jnp.conca...]
    dynamic_slice x0 -> x21, local copies, waits for them, and re-layouts: none -> 18.2 us  [the longest x17 11.7 us: halved(): sent = lax.dynamic_slice_in_dim(value, (1 - mine) * half, half, dim)]
  transfers between devices with their start and end apart: 13 -> 45, of which waited for: 8 -> 16; matrix products, arithmetic and copies ran while one was open for 15% -> 28% of each run, Pallas kernels for 12% -> 10%
where the time goes in v2:
time: 531 us; the launch traced here: 526 us
  Pallas kernels  151 us (28%)
  waiting for transfers between devices  133 us (25%)
  local copies, waits for them, and re-layouts  80.1 us (15%)
  other arithmetic  66.7 us (13%)
  starting transfers between devices  49.3 us (9%)
  matrix products  43.1 us (8%)
    ppermute x43, waiting for transfers between devices, swapped(): lax.ppermute(value, axis, [(i, i ^ 1 << bit) for i in range(lax.axis_size...  133 us
    pallas_call x1, Pallas kernels, middle(): pl.pallas_call(middle_kernel, grid=(steps,), in_specs=[fixed((rows, dim))...  58.8 us
    ppermute x43, starting transfers between devices, swapped(): lax.ppermute(value, axis, [(i, i ^ 1 << bit) for i in range(lax.axis_size...  46.1 us
    pallas_call x1, Pallas kernels, attend_back(): pl.pallas_call(partial(backward_kernel, ext=ext), grid=(micro, pairs), in...  38 us
    select_n x20, other arithmetic, doubled(): jnp.where(mine == 0, jnp.concatenate([value, other], axis=dim), jnp.conca...  28 us
    pallas_call x1, Pallas kernels, attend(): pl.pallas_call(partial(forward_kernel, ext=ext), grid=(micro, pairs), in_...  27.9 us
    pallas_call x1, Pallas kernels, spd_inverse(): pl.pallas_call(inverse_kernel, out_shape=jax.ShapeDtypeStruct(systems.sha...  26.7 us
    unnamed x149, local copies, waits for them, and re-layouts  24.5 us
  transfers between devices with their start and end apart: 45, of which 16 were waited for; matrix products, arithmetic and copies ran while one was open for 28% of the time, Pallas kernels for 10%

profile of v2, /device:TPU:0, one launch (start us, length us, event | category | flops | bytes accessed | tf_op | source)
XLA Modules:
  0.0 525.7 jit_solution(4184650153708771289)
XLA Ops:
  1.5 1.8 convolution_convert_fusion.3
  3.4 3.0 collective-permute-start.4
  14.1 2.3 constant_dynamic-slice_fusion.21
  16.4 2.0 collective-permute-start.1
  19.3 2.0 collective-permute-start.3
  24.2 26.7 %inverse.1 = f32[2,128,128]{2,1,0:T(8,128)} custom-call(f32[2,128,128]{2,1,0:T(8,128)} %convolution_add_fusion.1.a_ref), custom_call_target="tpu_custom_call" | custom-call | flops 25999998976 | bytes 300000 | tf_op jit(solution)/shard_map/inverse/pallas_call | solution.py:138
  50.9 2.1 fusion.58
  55.0 2.4 constant_dynamic-slice_fusion.17
  59.8 2.0 collective-permute-start.9
  74.5 36.1 %collective-permute-done.5 = bf16[192,768]{1,0:T(8,128)(2,1)S(1)} collective-permute-done((bf16[192,768]{1,0:T(8,128)(2,1)S(1)}, bf16[192,768]{1,0:T(8,128)(2,1)S(1)}, u32[]{:S(2)}, u32[]{:S(2)}) %collective-permute-start.5) | collective-permute-done | bytes 294944 | tf_op jit(solution)/shard_map/ppermute | solution.py:44
  116.6 2.0 maximum_select_fusion.8
  120.9 6.9 %convolution_convert_fusion.k_ref.v_ref = bf16[2,1024,1536]{2,1,0:T(8,128)(2,1)S(1)} fusion(bf16[768,2304]{1,0:T(8,128)(2,1)S(1)} %maximum_select_fusion.2, bf16[2,256,768]{2,1,0:T(8,128)(2,1)S(1)} %convolution_convert_fusion.2, bf16[2,512,768]{2,1,0:T(8,128)(2,1)S(1)} %fusion.7, bf16[2,256,768]{2,1,0:T(8,128)(2,1)S(1)} %fusion.23), kind=kOutput, calls=%fused_computation | convolution fusion | flops 4844421120 | bytes 11796480 | tf_op jit(solution)/shard_map/mtd,de->mte/dot_general | solution.py:542
  136.8 3.2 concatenate.168.st_ref
  140.0 27.9 %attend.1 = (bf16[2,512,768]{2,1,0:T(8,128)(2,1)}, bf16[2,12,2,256,512]{4,3,2,1,0:T(8,128)(2,1)}, bf16[2,12,512,256]{3,2,1,0:T(8,128)(2,1)}) custom-call(bf16[2,512,768]{2,1,0:T(8,128)(2,1)} %copy-done.20, bf16[2,1024,1536]{2,1,0:T(8,128)(2,1)} %copy-done.30, bf16[2,1024,1536]{2,1,0:T(8,128)(2,1)} %copy-done.30, s32[2,768,1]{2,1,0:T(8,128)} %copy.116.dcol_ref, ...), custom_call_target="tpu_custom_call" | custom-call | flops 28991029248 | bytes 30000000 | tf_op jit(solution)/shard_map/attend/pallas_call | solution.py:398
  169.1 2.8 maximum_select_fusion.3
  172.2 4.0 maximum_select_fusion.wfc_ref
  176.2 2.8 maximum_select_fusion.4
  179.3 3.2 maximum_select_fusion.1.wproj_ref
  182.4 58.8 %middle.1 = (bf16[1024,768]{1,0:T(8,128)(2,1)}, f32[1024,768]{1,0:T(8,128)}, bf16[1024,768]{1,0:T(8,128)(2,1)}, bf16[768,768]{1,0:T(8,128)(2,1)}, bf16[2,6,384,5...) custom-call(bf16[1024,768]{1,0:T(8,128)(2,1)} %bitcast.107, ...), custom_call_target="tpu_custom_call" | custom-call | flops 57982058496 | bytes 40000000 | tf_op jit(solution)/shard_map/middle/pallas_call | solution.py:343
  241.2 38.0 %attend_back.1 = (bf16[2,512,768]{2,1,0:T(8,128)(2,1)}, bf16[2,1024,768]{2,1,0:T(8,128)(2,1)}, bf16[2,1024,768]{2,1,0:T(8,128)(2,1)}, f32[2,8,768]{2,1,0:T(8,128)}) custom-call(bf16[2,512,768]{2,1,0:T(8,128)(2,1)} %bitcast.142, bf16[2,512,768]{2,1,0:T(8,128)(2,1)} %copy-done.20, bf16[2,1024,1536]{2,1,0:T(8,128)(2,1)} %copy-done.30, ...), custom_call_target="tpu_custom_call" | custom-call | flops 38654705664 | bytes 30000000 | tf_op jit(solution)/shard_map/attend_back/pallas_call | solution.py:437
  279.3 4.8 fusion.33
  284.1 2.7 convolution_add_fusion
  290.9 3.7 bitcast_convert_fusion.1
  294.6 3.7 bitcast_convert_fusion
  299.3 1.7 fusion.27
  304.3 2.7 collective-permute-start.11
  315.1 3.2 constant_dynamic-slice_fusion.5
  318.4 3.4 constant_dynamic-slice_fusion.10
  326.5 1.9 copy-done.2
  328.5 2.9 fusion.36
  331.6 5.2 fusion.13
  337.1 2.9 dynamic-slice_add_fusion
  341.6 2.1 collective-permute-start.32
  343.6 3.0 dynamic-slice_add_fusion.1
  349.5 2.2 dynamic-slice_add_fusion.2
  355.6 20.9 %collective-permute-done.42 = f32[6528]{0:T(1024)S(1)} collective-permute-done((f32[6528]{0:T(1024)S(1)}, f32[6528]{0:T(1024)S(1)}, u32[]{:S(2)}, u32[]{:S(2)}) %collective-permute-start.42) | collective-permute-done | bytes 26144 | tf_op jit(solution)/shard_map/ppermute | solution.py:44
  376.4 1.6 collective-permute-start.43
  378.1 1.7 dynamic-slice_add_fusion.3
  383.7 12.2 %collective-permute-done.14 = bf16[1,768,768]{2,1,0:T(8,128)(2,1)} collective-permute-done((bf16[1,768,768]{2,1,0:T(8,128)(2,1)}, bf16[1,768,768]{2,1,0:T(8,128)(2,1)}, u32[]{:S(2)}, u32[]{:S(2)}) %collective-permute-start.14) | collective-permute-done | bytes 1179680 | tf_op jit(solution)/shard_map/ppermute | solution.py:44
  399.1 1.6 collective-permute-start.34
  400.8 7.0 %collective-permute-done.24 = bf16[1,576,512]{2,1,0:T(8,128)(2,1)S(1)} collective-permute-done((bf16[1,576,512]{2,1,0:T(8,128)(2,1)S(1)}, bf16[1,576,512]{2,1,0:T(8,128)(2,1)S(1)}, u32[]{:S(2)}, u32[]{:S(2)}) %collective-permute-start.24) | collective-permute-done | bytes 589856 | tf_op jit(solution)/shard_map/ppermute | solution.py:44
  409.5 2.0 collective-permute-done.15
  413.4 4.5 collective-permute-done.25
  418.0 2.6 collective-permute-start.26
  420.6 5.2 collective-permute-done.16
  427.0 2.1 collective-permute-start.27
  430.2 11.3 %collective-permute-done.27 = bf16[144,512]{1,0:T(8,128)(2,1)S(1)} collective-permute-done((bf16[144,512]{1,0:T(8,128)(2,1)S(1)}, bf16[144,512]{1,0:T(8,128)(2,1)S(1)}, u32[]{:S(2)}, u32[]{:S(2)}) %collective-permute-start.27) | collective-permute-done | bytes 147488 | tf_op jit(solution)/shard_map/ppermute | solution.py:44
  441.6 3.2 collective-permute-start.28
  444.8 3.5 collective-permute-start.18
  448.5 8.2 %collective-permute-done.28 = bf16[288,512]{1,0:T(8,128)(2,1)S(1)} collective-permute-done((bf16[288,512]{1,0:T(8,128)(2,1)S(1)}, bf16[288,512]{1,0:T(8,128)(2,1)S(1)}, u32[]{:S(2)}, u32[]{:S(2)}) %collective-permute-start.28) | collective-permute-done | bytes 294944 | tf_op jit(solution)/shard_map/ppermute | solution.py:44
  458.7 2.8 collective-permute-start.44
  461.6 7.2 %collective-permute-done.19 = bf16[192,768]{1,0:T(8,128)(2,1)S(1)} collective-permute-done((bf16[192,768]{1,0:T(8,128)(2,1)S(1)}, bf16[192,768]{1,0:T(8,128)(2,1)S(1)}, u32[]{:S(2)}, u32[]{:S(2)}) %collective-permute-start.19) | collective-permute-done | bytes 294944 | tf_op jit(solution)/shard_map/ppermute | solution.py:44
  469.5 3.7 collective-permute-done.29
  473.8 2.5 fusion.12
  481.1 3.1 collective-permute-done.20
  486.5 8.6 %collective-permute-done.38 = bf16[384,768]{1,0:T(8,128)(2,1)} collective-permute-done((bf16[384,768]{1,0:T(8,128)(2,1)}, bf16[384,768]{1,0:T(8,128)(2,1)}, u32[]{:S(2)}, u32[]{:S(2)}) %collective-permute-start.38) | collective-permute-done | bytes 589856 | tf_op jit(solution)/shard_map/ppermute | solution.py:44
  495.1 2.9 maximum_select_fusion.12
  498.0 2.1 maximum_select_fusion.6
  500.1 2.9 convert_bitcast_fusion
  503.0 6.1 %copy.128 = f32[384,6,512]{0,2,1:T(8,128)} copy(f32[384,6,512]{2,0,1:T(8,128)} %convert_bitcast_fusion) | data formatting | bytes 9437184 | tf_op jit(solution)/shard_map/convert_element_type | solution.py:678
  509.1 6.0 %copy.133 = f32[384,3072]{1,0:T(8,128)} copy(f32[384,3072]{0,1:T(8,128)} %bitcast.113) | data formatting | bytes 9437184
  515.1 1.9 maximum_select_fusion.5
  518.3 2.0 maximum_convert_fusion
  520.3 5.1 fusion.17
  (346 shorter events, 102.7 us)
Async XLA Ops:
  0.6 17.7 %copy-start = (bf16[2,1,512,768]{3,2,1,0:T(8,128)(2,1)S(1)}, bf16[2,1,512,768]{3,2,1,0:T(8,128)(2,1)}, u32[]{:S(2)}) copy-start(bf16[2,1,512,768]{3,2,1,0:T(8,128)(2,1)} %param.16) | copy-start | bytes 4718596
  3.4 70.7 %collective-permute-start.4 = (bf16[2,64,768]{2,1,0:T(8,128)(2,1)S(1)}, bf16[2,64,768]{2,1,0:T(8,128)(2,1)S(1)}, u32[]{:S(2)}, u32[]{:S(2)}) collective-permute-start(bf16[2,64,768]{2,1,0:T(8,128)(2,1)S(1)} %convolution_convert_fusion.3), channel_id=1, source_target_pairs={{0,1},{1,0},{2,3},{3,2},{4,5},{5,4},{6,7},{7,6},{8,9},{9,8},{10,11... | collective-permute-start | bytes 589832 | tf_op jit(solution)/shard_map/ppermute | solution.py:44
  14.0 45.8 %collective-permute-start = (bf16[1,6528]{1,0:T(2,128)(2,1)S(1)}, bf16[1,6528]{1,0:T(2,128)(2,1)S(1)}, u32[]{:S(2)}, u32[]{:S(2)}) collective-permute-start(bf16[1,6528]{1,0:T(2,128)(2,1)S(1)} %broadcast_in_dim.16), channel_id=1, source_target_pairs={{0,1},{1,0},{2,3},{3,2},{4,5},{5,4},{6,7},{7,6},{8,9},{9,8},{10,11... | collective-permute-start | bytes 39176 | tf_op jit(solution)/shard_map/ppermute | solution.py:44
  16.4 97.5 %collective-permute-start.1 = (bf16[192,2304]{1,0:T(8,128)(2,1)}, bf16[192,2304]{1,0:T(8,128)(2,1)}, u32[]{:S(2)}, u32[]{:S(2)}) collective-permute-start(bf16[192,2304]{1,0:T(8,128)(2,1)} %constant_dynamic-slice_fusion.21), channel_id=1, source_target_pairs={{0,1},{1,0},{2,3},{3,2},{4,5},{5,4},{6,7},{7,6},{8,9},{9,8},{10,11... | collective-permute-start | bytes 2654216 | tf_op jit(solution)/shard_map/ppermute | solution.py:44
  19.3 94.7 %collective-permute-start.3 = (bf16[2,256,768]{2,1,0:T(8,128)(2,1)}, bf16[2,256,768]{2,1,0:T(8,128)(2,1)S(1)}, u32[]{:S(2)}, u32[]{:S(2)}) collective-permute-start(bf16[2,256,768]{2,1,0:T(8,128)(2,1)} %slice.175), channel_id=1, source_target_pairs={{0,1},{2,3},{4,5},{6,7},{8,9},{10,11},{12,13},{14,15},{16,17},{18,... | collective-permute-start | bytes 2359304 | tf_op jit(solution)/shard_map/ppermute | solution.py:502
  22.4 92.6 %collective-permute-start.7 = (bf16[192,3072]{1,0:T(8,128)(2,1)}, bf16[192,3072]{1,0:T(8,128)(2,1)}, u32[]{:S(2)}, u32[]{:S(2)}) collective-permute-start(bf16[192,3072]{1,0:T(8,128)(2,1)} %constant_dynamic-slice_fusion.18), channel_id=1, source_target_pairs={{0,1},{1,0},{2,3},{3,2},{4,5},{5,4},{6,7},{7,6},{8,9},{9,8},{10,11... | collective-permute-start | bytes 3538952 | tf_op jit(solution)/shard_map/ppermute | solution.py:44
  22.7 30.8 %copy-start.39 = (s32[768]{0:T(1024)}, s32[768]{0:T(1024)S(1)}, u32[]{:S(2)}) copy-start(s32[768]{0:T(1024)S(1)} %add_select_fusion) | copy-start | bytes 9220
  24.2 30.0 %copy-start.50 = (s32[2,1,1024]{2,1,0:T(1,128)S(1)}, s32[2,1,1024]{2,1,0:T(1,128)}, u32[]{:S(2)}) copy-start(s32[2,1,1024]{2,1,0:T(1,128)} %param.18) | copy-start | bytes 24580
  24.2 30.0 %copy-start.21 = (bf16[384,768]{1,0:T(8,128)(2,1)S(1)}, bf16[384,768]{1,0:T(8,128)(2,1)}, u32[]{:S(2)}) copy-start(bf16[384,768]{1,0:T(8,128)(2,1)} %param.21) | copy-start | bytes 1769476
  53.0 19.8 %copy-start.33 = (f32[2,512]{1,0:T(2,128)}, f32[2,512]{1,0:T(2,128)S(1)}, u32[]{:S(2)}) copy-start(f32[2,512]{1,0:T(2,128)S(1)} %broadcast_multiply_fusion.6) | copy-start | bytes 12292
  53.6 19.1 %copy-start.37 = (f32[2,512]{1,0:T(2,128)}, f32[2,512]{1,0:T(2,128)S(1)}, u32[]{:S(2)}) copy-start(f32[2,512]{1,0:T(2,128)S(1)} %add_rsqrt_fusion) | copy-start | bytes 12292
  59.8 55.7 %collective-permute-start.9 = (bf16[768,768]{1,0:T(8,128)(2,1)}, bf16[768,768]{1,0:T(8,128)(2,1)}, u32[]{:S(2)}, u32[]{:S(2)}) collective-permute-start(bf16[768,768]{1,0:T(8,128)(2,1)} %constant_dynamic-slice_fusion.17), channel_id=1, source_target_pairs={{0,1},{1,0},{2,3},{3,2},{4,5},{5,4},{6,7},{7,6},{8,9},{9,8},{10,11... | collective-permute-start | bytes 3538952 | tf_op jit(solution)/shard_map/ppermute | solution.py:44
  63.1 51.5 %copy-start.35 = (f32[768]{0:T(1024)}, f32[768]{0:T(1024)S(1)}, u32[]{:S(2)}) copy-start(f32[768]{0:T(1024)S(1)} %reshape.368) | copy-start | bytes 9220
  72.7 37.9 %copy-start.26 = (f32[2,256,128]{2,1,0:T(8,128)S(1)}, f32[2,256,128]{2,1,0:T(8,128)}, u32[]{:S(2)}) copy-start(f32[2,256,128]{2,1,0:T(8,128)} %fusion.58) | copy-start | bytes 786436
  73.4 47.5 %copy-start.18 = (bf16[2,512,768]{2,1,0:T(8,128)(2,1)}, bf16[2,512,768]{2,1,0:T(8,128)(2,1)S(1)}, u32[]{:S(2)}) copy-start(bf16[2,512,768]{2,1,0:T(8,128)(2,1)S(1)} %fusion.7) | copy-start | bytes 4718596
  73.4 39.1 %copy-start.22 = (bf16[384,768]{1,0:T(8,128)(2,1)S(1)}, bf16[384,768]{1,0:T(8,128)(2,1)}, u32[]{:S(2)}) copy-start(bf16[384,768]{1,0:T(8,128)(2,1)} %param.21) | copy-start | bytes 1769476
  74.1 36.6 %collective-permute-start.5 = (bf16[192,768]{1,0:T(8,128)(2,1)S(1)}, bf16[192,768]{1,0:T(8,128)(2,1)S(1)}, u32[]{:S(2)}, u32[]{:S(2)}) collective-permute-start(bf16[192,768]{1,0:T(8,128)(2,1)S(1)} %copy-done.31), channel_id=1, source_target_pairs={{0,1},{1,0},{2,3},{3,2},{4,5},{5,4},{6,7},{7,6},{8,9},{9,8},{10,11... | collective-permute-start | bytes 884744 | tf_op jit(solution)/shard_map/ppermute | solution.py:44
  110.7 1.6 collective-permute-start.6
  111.6 9.3 %copy-start.54 = (bf16[2,256,768]{2,1,0:T(8,128)(2,1)}, bf16[2,256,768]{2,1,0:T(8,128)(2,1)S(1)}, u32[]{:S(2)}) copy-start(bf16[2,256,768]{2,1,0:T(8,128)(2,1)S(1)} %convolution_convert_fusion.2) | copy-start | bytes 2359300
  113.9 2.6 collective-permute-start.2
  115.0 54.1 %collective-permute-start.8 = (bf16[192,3072]{1,0:T(8,128)(2,1)}, bf16[192,3072]{1,0:T(8,128)(2,1)}, u32[]{:S(2)}, u32[]{:S(2)}) collective-permute-start(bf16[192,3072]{1,0:T(8,128)(2,1)} %collective-permute-done.7), channel_id=1, source_target_pairs={{0,2},{2,0},{4,6},{6,4},{8,10},{10,8},{12,14},{14,12},{16,18},{18,... | collective-permute-start | bytes 3538952 | tf_op jit(solution)/shard_map/ppermute | solution.py:44
  115.5 60.7 %collective-permute-start.10 = (bf16[768,768]{1,0:T(8,128)(2,1)}, bf16[768,768]{1,0:T(8,128)(2,1)}, u32[]{:S(2)}, u32[]{:S(2)}) collective-permute-start(bf16[768,768]{1,0:T(8,128)(2,1)} %collective-permute-done.9), channel_id=1, source_target_pairs={{0,2},{2,0},{4,6},{6,4},{8,10},{10,8},{12,14},{14,12},{16,18},{18,... | collective-permute-start | bytes 3538952 | tf_op jit(solution)/shard_map/ppermute | solution.py:44
  119.5 164.6 %copy-start.14 = (bf16[768,2304]{1,0:T(8,128)(2,1)}, bf16[768,2304]{1,0:T(8,128)(2,1)S(1)}, u32[]{:S(2)}) copy-start(bf16[768,2304]{1,0:T(8,128)(2,1)S(1)} %maximum_select_fusion.2) | copy-start | bytes 10616836
  120.9 7.8 %copy-start.20 = (bf16[2,512,768]{2,1,0:T(8,128)(2,1)}, bf16[2,512,768]{2,1,0:T(8,128)(2,1)S(1)}, u32[]{:S(2)}) copy-start(bf16[2,512,768]{2,1,0:T(8,128)(2,1)S(1)} %convolution_convert_fusion.1.q_ref) | copy-start | bytes 4718596
  286.7 7.9 %copy-start.12 = (f32[2,1024,768]{2,1,0:T(8,128)}, f32[2,1024,768]{2,1,0:T(8,128)S(1)}, u32[]{:S(2)}) copy-start(f32[2,1024,768]{2,1,0:T(8,128)S(1)} %convolution_add_fusion) | copy-start | bytes 18874372
  302.3 29.2 %collective-permute-start.12 = (bf16[2,256,768]{2,1,0:T(8,128)(2,1)}, bf16[2,256,768]{2,1,0:T(8,128)(2,1)S(1)}, u32[]{:S(2)}, u32[]{:S(2)}) collective-permute-start(bf16[2,256,768]{2,1,0:T(8,128)(2,1)} %slice.263), channel_id=1, source_target_pairs={{1,0},{3,2},{5,4},{7,6},{9,8},{11,10},{13,12},{15,14},{17,16},{19,... | collective-permute-start | bytes 2359304 | tf_op jit(solution)/shard_map/ppermute | solution.py:623
  304.3 27.2 %collective-permute-start.11 = (bf16[2,64,768]{2,1,0:T(8,128)(2,1)}, bf16[2,64,768]{2,1,0:T(8,128)(2,1)}, u32[]{:S(2)}, u32[]{:S(2)}) collective-permute-start(bf16[2,64,768]{2,1,0:T(8,128)(2,1)} %constant_dynamic-slice_fusion.16), channel_id=1, source_target_pairs={{0,1},{1,0},{2,3},{3,2},{4,5},{5,4},{6,7},{7,6},{8,9},{9,8},{10,11... | collective-permute-start | bytes 589832 | tf_op jit(solution)/shard_map/ppermute | solution.py:44
  318.4 18.8 %collective-permute-start.31 = (bf16[2,768,768]{2,1,0:T(8,128)(2,1)}, bf16[2,768,768]{2,1,0:T(8,128)(2,1)}, u32[]{:S(2)}, u32[]{:S(2)}) collective-permute-start(bf16[2,768,768]{2,1,0:T(8,128)(2,1)} %constant_dynamic-slice_fusion.5), channel_id=1, source_target_pairs={{0,2},{2,0},{4,6},{6,4},{8,10},{10,8},{12,14},{14,12},{16,18},{18,... | collective-permute-start | bytes 7077896 | tf_op jit(solution)/shard_map/ppermute | solution.py:44
  321.8 21.9 %collective-permute-start.22 = (bf16[2,1152,512]{2,1,0:T(8,128)(2,1)}, bf16[2,1152,512]{2,1,0:T(8,128)(2,1)}, u32[]{:S(2)}, u32[]{:S(2)}) collective-permute-start(bf16[2,1152,512]{2,1,0:T(8,128)(2,1)} %constant_dynamic-slice_fusion.10), channel_id=1, source_target_pairs={{0,2},{2,0},{4,6},{6,4},{8,10},{10,8},{12,14},{14,12},{16,18},{18,... | collective-permute-start | bytes 7077896 | tf_op jit(solution)/shard_map/ppermute | solution.py:44
  328.4 21.0 %collective-permute-start.13 = (bf16[2,768,768]{2,1,0:T(8,128)(2,1)}, bf16[2,768,768]{2,1,0:T(8,128)(2,1)}, u32[]{:S(2)}, u32[]{:S(2)}) collective-permute-start(bf16[2,768,768]{2,1,0:T(8,128)(2,1)} %constant_dynamic-slice_fusion.15), channel_id=1, source_target_pairs={{0,2},{2,0},{4,6},{6,4},{8,10},{10,8},{12,14},{14,12},{16,18},{18,... | collective-permute-start | bytes 7077896 | tf_op jit(solution)/shard_map/ppermute | solution.py:44
  337.0 16.7 %collective-permute-start.40 = (f32[1,6528]{1,0:T(1,128)S(1)}, f32[1,6528]{1,0:T(1,128)S(1)}, u32[]{:S(2)}, u32[]{:S(2)}) collective-permute-start(f32[1,6528]{1,0:T(1,128)S(1)} %constant_dynamic-slice_fusion), channel_id=1, source_target_pairs={{0,1},{1,0},{2,3},{3,2},{4,5},{5,4},{6,7},{7,6},{8,9},{9,8},{10,11... | collective-permute-start | bytes 78344 | tf_op jit(solution)/shard_map/ppermute | solution.py:44
  341.5 8.0 %slice-start = ((s8[4718592]{0:T(1024)(128)(4,1)}), s8[4194304]{0:T(1024)(128)(4,1)S(1)}, s32[]{:S(2)}) async-start(s8[4718592]{0:T(1024)(128)(4,1)} %bitcast.110), calls=%async_computation | async-start | bytes 8388608
  341.6 7.9 %slice-start.1 = ((s8[4718592]{0:T(1024)(128)(4,1)}), s8[524288]{0:T(1024)(128)(4,1)S(1)}, s32[]{:S(2)}) async-start(s8[4718592]{0:T(1024)(128)(4,1)} %bitcast.110), calls=%async_computation.1 | async-start | bytes 1048576
  341.6 36.5 %collective-permute-start.32 = (bf16[1,768,768]{2,1,0:T(8,128)(2,1)S(1)}, bf16[1,768,768]{2,1,0:T(8,128)(2,1)}, u32[]{:S(2)}, u32[]{:S(2)}) collective-permute-start(bf16[1,768,768]{2,1,0:T(8,128)(2,1)S(1)} %constant_dynamic-slice_fusion.4), channel_id=1, source_target_pairs={{0,1},{1,0},{2,3},{3,2},{4,5},{5,4},{6,7},{7,6},{8,9},{9,8},{10,11... | collective-permute-start | bytes 3538952 | tf_op jit(solution)/shard_map/ppermute | solution.py:44
  347.9 33.6 %collective-permute-start.23 = (bf16[2,576,512]{2,1,0:T(8,128)(2,1)}, bf16[2,576,512]{2,1,0:T(8,128)(2,1)}, u32[]{:S(2)}, u32[]{:S(2)}) collective-permute-start(bf16[2,576,512]{2,1,0:T(8,128)(2,1)} %constant_dynamic-slice_fusion.9), channel_id=1, source_target_pairs={{0,4},{2,6},{4,0},{6,2},{8,12},{10,14},{12,8},{14,10},{16,20},{18,... | collective-permute-start | bytes 3538952 | tf_op jit(solution)/shard_map/ppermute | solution.py:44
  353.5 42.4 %collective-permute-start.14 = (bf16[1,768,768]{2,1,0:T(8,128)(2,1)}, bf16[1,768,768]{2,1,0:T(8,128)(2,1)}, u32[]{:S(2)}, u32[]{:S(2)}) collective-permute-start(bf16[1,768,768]{2,1,0:T(8,128)(2,1)} %constant_dynamic-slice_fusion.14), channel_id=1, source_target_pairs={{0,1},{1,0},{2,3},{3,2},{4,5},{5,4},{6,7},{7,6},{8,9},{9,8},{10,11... | collective-permute-start | bytes 3538952 | tf_op jit(solution)/shard_map/ppermute | solution.py:44
  353.8 1.3 collective-permute-start.41
  355.1 21.4 %collective-permute-start.42 = (f32[6528]{0:T(1024)S(1)}, f32[6528]{0:T(1024)S(1)}, u32[]{:S(2)}, u32[]{:S(2)}) collective-permute-start(f32[6528]{0:T(1024)S(1)} %add.350), channel_id=1, source_target_pairs={{0,4},{2,6},{4,0},{6,2},{8,12},{10,14},{12,8},{14,10},{16,20},{18,... | collective-permute-start | bytes 78344 | tf_op jit(solution)/shard_map/ppermute | solution.py:44
  376.4 82.2 %collective-permute-start.43 = (f32[6528]{0:T(1024)S(1)}, f32[6528]{0:T(1024)S(1)}, u32[]{:S(2)}, u32[]{:S(2)}) collective-permute-start(f32[6528]{0:T(1024)S(1)} %add.351), channel_id=1, source_target_pairs={{0,8},{2,10},{4,12},{6,14},{8,0},{10,2},{12,4},{14,6},{16,24},{18,... | collective-permute-start | bytes 78344 | tf_op jit(solution)/shard_map/ppermute | solution.py:44
  379.9 16.0 %copy-start.8 = (bf16[2,768,768]{2,1,0:T(8,128)(2,1)S(1)}, bf16[2,768,768]{2,1,0:T(8,128)(2,1)}, u32[]{:S(2)}) copy-start(bf16[2,768,768]{2,1,0:T(8,128)(2,1)} %copy-done.7) | copy-start | bytes 7077892
  379.9 19.1 %collective-permute-start.33 = (bf16[1,384,768]{2,1,0:T(8,128)(2,1)S(1)}, bf16[1,384,768]{2,1,0:T(8,128)(2,1)S(1)}, u32[]{:S(2)}, u32[]{:S(2)}) collective-permute-start(bf16[1,384,768]{2,1,0:T(8,128)(2,1)S(1)} %constant_dynamic-slice_fusion.3), channel_id=1, source_target_pairs={{0,4},{2,6},{4,0},{6,2},{8,12},{10,14},{12,8},{14,10},{16,20},{18,... | collective-permute-start | bytes 1769480 | tf_op jit(solution)/shard_map/ppermute | solution.py:44
  383.1 24.6 %collective-permute-start.24 = (bf16[1,576,512]{2,1,0:T(8,128)(2,1)S(1)}, bf16[1,576,512]{2,1,0:T(8,128)(2,1)S(1)}, u32[]{:S(2)}, u32[]{:S(2)}) collective-permute-start(bf16[1,576,512]{2,1,0:T(8,128)(2,1)S(1)} %constant_dynamic-slice_fusion.8), channel_id=1, source_target_pairs={{0,1},{1,0},{2,3},{3,2},{4,5},{5,4},{6,7},{7,6},{8,9},{9,8},{10,11... | collective-permute-start | bytes 1769480 | tf_op jit(solution)/shard_map/ppermute | solution.py:44
  397.4 14.2 %collective-permute-start.15 = (bf16[1,384,768]{2,1,0:T(8,128)(2,1)S(1)}, bf16[1,384,768]{2,1,0:T(8,128)(2,1)S(1)}, u32[]{:S(2)}, u32[]{:S(2)}) collective-permute-start(bf16[1,384,768]{2,1,0:T(8,128)(2,1)S(1)} %constant_dynamic-slice_fusion.13), channel_id=1, source_target_pairs={{0,4},{2,6},{4,0},{6,2},{8,12},{10,14},{12,8},{14,10},{16,20},{18,... | collective-permute-start | bytes 1769480 | tf_op jit(solution)/shard_map/ppermute | solution.py:44
  399.1 29.9 %collective-permute-start.34 = (bf16[1,192,768]{2,1,0:T(8,128)(2,1)S(1)}, bf16[1,192,768]{2,1,0:T(8,128)(2,1)S(1)}, u32[]{:S(2)}, u32[]{:S(2)}) collective-permute-start(bf16[1,192,768]{2,1,0:T(8,128)(2,1)S(1)} %constant_dynamic-slice_fusion.2), channel_id=1, source_target_pairs={{0,8},{2,10},{4,12},{6,14},{8,0},{10,2},{12,4},{14,6},{16,24},{18,... | collective-permute-start | bytes 884744 | tf_op jit(solution)/shard_map/ppermute | solution.py:44
  407.9 9.9 %collective-permute-start.25 = (bf16[1,288,512]{2,1,0:T(8,128)(2,1)S(1)}, bf16[1,288,512]{2,1,0:T(8,128)(2,1)S(1)}, u32[]{:S(2)}, u32[]{:S(2)}) collective-permute-start(bf16[1,288,512]{2,1,0:T(8,128)(2,1)S(1)} %constant_dynamic-slice_fusion.7), channel_id=1, source_target_pairs={{0,8},{2,10},{4,12},{6,14},{8,0},{10,2},{12,4},{14,6},{16,24},{18,... | collective-permute-start | bytes 884744 | tf_op jit(solution)/shard_map/ppermute | solution.py:44
  411.7 14.1 %collective-permute-start.16 = (bf16[1,192,768]{2,1,0:T(8,128)(2,1)S(1)}, bf16[1,192,768]{2,1,0:T(8,128)(2,1)S(1)}, u32[]{:S(2)}, u32[]{:S(2)}) collective-permute-start(bf16[1,192,768]{2,1,0:T(8,128)(2,1)S(1)} %constant_dynamic-slice_fusion.12), channel_id=1, source_target_pairs={{0,8},{2,10},{4,12},{6,14},{8,0},{10,2},{12,4},{14,6},{16,24},{18,... | collective-permute-start | bytes 884744 | tf_op jit(solution)/shard_map/ppermute | solution.py:44
  418.0 9.0 %collective-permute-start.26 = (bf16[1,144,512]{2,1,0:T(8,128)(2,1)S(1)}, bf16[1,144,512]{2,1,0:T(8,128)(2,1)S(1)}, u32[]{:S(2)}, u32[]{:S(2)}) collective-permute-start(bf16[1,144,512]{2,1,0:T(8,128)(2,1)S(1)} %constant_dynamic-slice_fusion.6), channel_id=1, source_target_pairs={{0,16},{2,18},{4,20},{6,22},{8,24},{10,26},{12,28},{14,30},{16,0},... | collective-permute-start | bytes 442376 | tf_op jit(solution)/shard_map/ppermute | solution.py:44
  426.0 18.8 %collective-permute-start.17 = (bf16[1,96,768]{2,1,0:T(8,128)(2,1)S(1)}, bf16[1,96,768]{2,1,0:T(8,128)(2,1)S(1)}, u32[]{:S(2)}, u32[]{:S(2)}) collective-permute-start(bf16[1,96,768]{2,1,0:T(8,128)(2,1)S(1)} %constant_dynamic-slice_fusion.11), channel_id=1, source_target_pairs={{0,16},{2,18},{4,20},{6,22},{8,24},{10,26},{12,28},{14,30},{16,0},... | collective-permute-start | bytes 442376 | tf_op jit(solution)/shard_map/ppermute | solution.py:44
  427.0 14.5 %collective-permute-start.27 = (bf16[144,512]{1,0:T(8,128)(2,1)S(1)}, bf16[144,512]{1,0:T(8,128)(2,1)S(1)}, u32[]{:S(2)}, u32[]{:S(2)}) collective-permute-start(bf16[144,512]{1,0:T(8,128)(2,1)S(1)} %add_bitcast_fusion.1), channel_id=1, source_target_pairs={{0,16},{2,18},{4,20},{6,22},{8,24},{10,26},{12,28},{14,30},{16,0},... | collective-permute-start | bytes 442376 | tf_op jit(solution)/shard_map/ppermute | solution.py:44
  429.2 19.2 %collective-permute-start.35 = (bf16[1,96,768]{2,1,0:T(8,128)(2,1)S(1)}, bf16[1,96,768]{2,1,0:T(8,128)(2,1)S(1)}, u32[]{:S(2)}, u32[]{:S(2)}) collective-permute-start(bf16[1,96,768]{2,1,0:T(8,128)(2,1)S(1)} %constant_dynamic-slice_fusion.1), channel_id=1, source_target_pairs={{0,16},{2,18},{4,20},{6,22},{8,24},{10,26},{12,28},{14,30},{16,0},... | collective-permute-start | bytes 442376 | tf_op jit(solution)/shard_map/ppermute | solution.py:44
  441.6 15.1 %collective-permute-start.28 = (bf16[288,512]{1,0:T(8,128)(2,1)S(1)}, bf16[288,512]{1,0:T(8,128)(2,1)S(1)}, u32[]{:S(2)}, u32[]{:S(2)}) collective-permute-start(bf16[288,512]{1,0:T(8,128)(2,1)S(1)} %maximum_select_fusion.19), channel_id=1, source_target_pairs={{0,8},{2,10},{4,12},{6,14},{8,0},{10,2},{12,4},{14,6},{16,24},{18,... | collective-permute-start | bytes 884744 | tf_op jit(solution)/shard_map/ppermute | solution.py:44
  444.8 13.7 %collective-permute-start.18 = (bf16[96,768]{1,0:T(8,128)(2,1)S(1)}, bf16[96,768]{1,0:T(8,128)(2,1)S(1)}, u32[]{:S(2)}, u32[]{:S(2)}) collective-permute-start(bf16[96,768]{1,0:T(8,128)(2,1)S(1)} %add_bitcast_fusion.2), channel_id=1, source_target_pairs={{0,16},{2,18},{4,20},{6,22},{8,24},{10,26},{12,28},{14,30},{16,0},... | collective-permute-start | bytes 442376 | tf_op jit(solution)/shard_map/ppermute | solution.py:44
  448.3 25.4 %copy-start.17 = (f32[1024,768]{1,0:T(8,128)S(1)}, f32[1024,768]{1,0:T(8,128)}, u32[]{:S(2)}) copy-start(f32[1024,768]{1,0:T(8,128)} %get-tuple-element.31) | copy-start | bytes 9437188
  448.4 13.1 %collective-permute-start.36 = (bf16[96,768]{1,0:T(8,128)(2,1)S(1)}, bf16[96,768]{1,0:T(8,128)(2,1)S(1)}, u32[]{:S(2)}, u32[]{:S(2)}) collective-permute-start(bf16[96,768]{1,0:T(8,128)(2,1)S(1)} %add_bitcast_fusion), channel_id=1, source_target_pairs={{0,16},{2,18},{4,20},{6,22},{8,24},{10,26},{12,28},{14,30},{16,0},... | collective-permute-start | bytes 442376 | tf_op jit(solution)/shard_map/ppermute | solution.py:44
  456.9 16.9 %copy-start.3 = (f32[2,512,768]{2,1,0:T(8,128)S(1)}, f32[2,512,768]{2,1,0:T(8,128)}, u32[]{:S(2)}) copy-start(f32[2,512,768]{2,1,0:T(8,128)} %get-tuple-element.143) | copy-start | bytes 9437188
  456.9 16.3 %collective-permute-start.29 = (bf16[576,512]{1,0:T(8,128)(2,1)S(1)}, bf16[576,512]{1,0:T(8,128)(2,1)S(1)}, u32[]{:S(2)}, u32[]{:S(2)}) collective-permute-start(bf16[576,512]{1,0:T(8,128)(2,1)S(1)} %maximum_select_fusion.15), channel_id=1, source_target_pairs={{0,4},{2,6},{4,0},{6,2},{8,12},{10,14},{12,8},{14,10},{16,20},{18,... | collective-permute-start | bytes 1769480 | tf_op jit(solution)/shard_map/ppermute | solution.py:44
  458.6 10.2 %collective-permute-start.19 = (bf16[192,768]{1,0:T(8,128)(2,1)S(1)}, bf16[192,768]{1,0:T(8,128)(2,1)S(1)}, u32[]{:S(2)}, u32[]{:S(2)}) collective-permute-start(bf16[192,768]{1,0:T(8,128)(2,1)S(1)} %maximum_select_fusion.18), channel_id=1, source_target_pairs={{0,8},{2,10},{4,12},{6,14},{8,0},{10,2},{12,4},{14,6},{16,24},{18,... | collective-permute-start | bytes 884744 | tf_op jit(solution)/shard_map/ppermute | solution.py:44
  458.7 17.7 %collective-permute-start.44 = (f32[6528]{0:T(1024)S(1)}, f32[6528]{0:T(1024)S(1)}, u32[]{:S(2)}, u32[]{:S(2)}) collective-permute-start(f32[6528]{0:T(1024)S(1)} %add.352), channel_id=1, source_target_pairs={{0,16},{2,18},{4,20},{6,22},{8,24},{10,26},{12,28},{14,30},{16,0},... | collective-permute-start | bytes 78344 | tf_op jit(solution)/shard_map/ppermute | solution.py:44
  461.5 14.9 %collective-permute-start.37 = (bf16[192,768]{1,0:T(8,128)(2,1)S(1)}, bf16[192,768]{1,0:T(8,128)(2,1)S(1)}, u32[]{:S(2)}, u32[]{:S(2)}) collective-permute-start(bf16[192,768]{1,0:T(8,128)(2,1)S(1)} %maximum_select_fusion.20), channel_id=1, source_target_pairs={{0,8},{2,10},{4,12},{6,14},{8,0},{10,2},{12,4},{14,6},{16,24},{18,... | collective-permute-start | bytes 884744 | tf_op jit(solution)/shard_map/ppermute | solution.py:44
  469.0 15.2 %collective-permute-start.20 = (bf16[384,768]{1,0:T(8,128)(2,1)S(1)}, bf16[384,768]{1,0:T(8,128)(2,1)}, u32[]{:S(2)}, u32[]{:S(2)}) collective-permute-start(bf16[384,768]{1,0:T(8,128)(2,1)S(1)} %maximum_select_fusion.14), channel_id=1, source_target_pairs={{0,4},{2,6},{4,0},{6,2},{8,12},{10,14},{12,8},{14,10},{16,20},{18,... | collective-permute-start | bytes 1769480 | tf_op jit(solution)/shard_map/ppermute | solution.py:44
  473.7 24.3 %collective-permute-start.30 = (bf16[1152,512]{1,0:T(8,128)(2,1)S(1)}, bf16[1152,512]{1,0:T(8,128)(2,1)}, u32[]{:S(2)}, u32[]{:S(2)}) collective-permute-start(bf16[1152,512]{1,0:T(8,128)(2,1)S(1)} %maximum_select_fusion.11), channel_id=1, source_target_pairs={{0,2},{2,0},{4,6},{6,4},{8,10},{10,8},{12,14},{14,12},{16,18},{18,... | collective-permute-start | bytes 3538952 | tf_op jit(solution)/shard_map/ppermute | solution.py:44
  477.4 17.7 %collective-permute-start.38 = (bf16[384,768]{1,0:T(8,128)(2,1)}, bf16[384,768]{1,0:T(8,128)(2,1)}, u32[]{:S(2)}, u32[]{:S(2)}) collective-permute-start(bf16[384,768]{1,0:T(8,128)(2,1)} %maximum_select_fusion.16), channel_id=1, source_target_pairs={{0,4},{2,6},{4,0},{6,2},{8,12},{10,14},{12,8},{14,10},{16,20},{18,... | collective-permute-start | bytes 1769480 | tf_op jit(solution)/shard_map/ppermute | solution.py:44
  485.8 29.3 %collective-permute-start.21 = (bf16[768,768]{1,0:T(8,128)(2,1)S(1)}, bf16[768,768]{1,0:T(8,128)(2,1)}, u32[]{:S(2)}, u32[]{:S(2)}) collective-permute-start(bf16[768,768]{1,0:T(8,128)(2,1)S(1)} %maximum_select_fusion.10), channel_id=1, source_target_pairs={{0,2},{2,0},{4,6},{6,4},{8,10},{10,8},{12,14},{14,12},{16,18},{18,... | collective-permute-start | bytes 3538952 | tf_op jit(solution)/shard_map/ppermute | solution.py:44
  498.0 22.3 %collective-permute-start.39 = (bf16[768,768]{1,0:T(8,128)(2,1)}, bf16[768,768]{1,0:T(8,128)(2,1)}, u32[]{:S(2)}, u32[]{:S(2)}) collective-permute-start(bf16[768,768]{1,0:T(8,128)(2,1)} %maximum_select_fusion.12), channel_id=1, source_target_pairs={{0,2},{2,0},{4,6},{6,4},{8,10},{10,8},{12,14},{14,12},{16,18},{18,... | collective-permute-start | bytes 3538952 | tf_op jit(solution)/shard_map/ppermute | solution.py:44
  (43 other events, 179.3 us)
